TPU v7x, 256 devices: a whole 4x4x8 slice. The times are simulated.
256 devices in a mesh: gx: 8 (over z_lo, x), gy: 4 (over z_hi), gz: 8 (over y, core).
Axes of the slice: x: 4, y: 4, z: 8 (z_hi: 4, z_lo: 2; z = z_hi * 2 + z_lo), core: 2. Of those that a mesh axis runs over, the one named last changes fastest.
Arguments:
- fields: bfloat16 [7, 64, 32, 128], P(None, 'gx', 'gy', 'gz'), may hold values from -6 to 6
- grain_ids: int32 [64, 32, 128], P('gx', 'gy', 'gz'), may hold values from 0 to 127
- material_table: bfloat16 [128, 64], replicated, may hold values from -6 to 6
- input_weight: bfloat16 [64, 7], replicated, may hold values from -2 to 2
- kernel_fine: bfloat16 [64, 1728], replicated, may hold values from -0.15625 to 0.15625
- kernel_down: bfloat16 [128, 1728], replicated, may hold values from -0.15625 to 0.15625
- kernel_bottle: bfloat16 [256, 3456], P('gx'), may hold values from -0.109375 to 0.109375
- cotangent: bfloat16 [256, 32, 16, 64], P('gx', None, 'gy', 'gz'), may hold values from -6 to 6
Outputs:
- bottle: bfloat16 [256, 32, 16, 64], P('gx', None, 'gy', 'gz')
- grad_down: float32 [128, 1728], P('gx', ('gy', 'gz'))
- grad_bottle: float32 [256, 3456], P('gx', ('gy', 'gz'))
Inputs may be any that keep to these rules, and one draw needn't show every extreme that they name: `grain_ids`: each voxel's grain, a row of material_table.
All inputs are finite; a program needn't handle non-finite values.
Results may differ from a plain program's by a relative error of at most 0.028.
Values may be sent and summed in bfloat16 or wider, within the bound.
A program may use at most 64 MiB of HBM per device.

v0:
```python
import math

import jax
import jax.numpy as jnp
from jax import lax
from jax.sharding import PartitionSpec as P


def with_halo(block, sides, width):
    for axis, dim in sides:
        count = lax.axis_size(axis)
        forward = [(i, i + 1) for i in range(count - 1)]
        backward = [(target, source) for source, target in forward]
        low = lax.ppermute(
            lax.slice_in_dim(block, block.shape[dim] - width, None, axis=dim), axis, forward
        )
        high = lax.ppermute(lax.slice_in_dim(block, 0, width, axis=dim), axis, backward)
        block = jnp.concatenate([low, block, high], axis=dim)
    return block


def laid_out(pieces, dim):
    pieces = jnp.moveaxis(pieces, 0, dim)
    shape = pieces.shape
    return pieces.reshape(*shape[:dim], shape[dim] * shape[dim + 1], *shape[dim + 2 :])


def copy_for_each(value, axis):
    count = lax.axis_size(axis)
    return lax.all_to_all(
        jnp.broadcast_to(value[None], (count, *value.shape)), axis, 0, 0, tiled=True
    )


def gathered_copies(value, axis, dim):
    return laid_out(copy_for_each(value, axis), dim)


def split_up(value, dim, count):
    before, after = (value.shape[:dim], value.shape[dim + 1 :])
    return jnp.moveaxis(value.reshape(*before, count, -1, *after), dim, 0)


def sum_at_owner(value, axis, dim):
    pieces = split_up(value, dim, lax.axis_size(axis))
    arrived = lax.all_to_all(pieces, axis, split_axis=0, concat_axis=0, tiled=True)
    return arrived.astype(jnp.float32).sum(axis=0)


def tap_offsets():
    offsets = []
    for along_x in range(3):
        for along_y in range(3):
            for along_z in range(3):
                offsets.append((along_x, along_y, along_z))
    return offsets


def silu_grad(values):
    sigmoid = jax.nn.sigmoid(values)
    return sigmoid * (1.0 + values * (1.0 - sigmoid))


def take_window(padded, offset, out_shape, stride):
    limits = (
        padded.shape[0],
        offset[0] + stride * (out_shape[0] - 1) + 1,
        offset[1] + stride * (out_shape[1] - 1) + 1,
        offset[2] + stride * (out_shape[2] - 1) + 1,
    )
    sliced = lax.slice(
        padded, (0, offset[0], offset[1], offset[2]), limits, (1, stride, stride, stride)
    )
    return sliced.reshape(padded.shape[0], -1)


def correlate(padded, kernel, out_shape, stride):
    channels = padded.shape[0]
    outputs = kernel.shape[0]
    kernel_taps = kernel.reshape(outputs, 27, channels)
    running = jnp.zeros((outputs, out_shape[0] * out_shape[1] * out_shape[2]), jnp.float32)
    for number, offset in enumerate(tap_offsets()):
        sliced = take_window(padded, offset, out_shape, stride)
        running = running + jnp.dot(
            kernel_taps[:, number], sliced, preferred_element_type=jnp.float32
        )
    return running.reshape((outputs,) + tuple(out_shape))


def transpose_correlate(padded, kernel, out_shape):
    outputs = kernel.shape[0]
    channels = kernel.shape[1] // 27
    kernel_taps = kernel.reshape(outputs, 27, channels)
    running = jnp.zeros((channels, out_shape[0] * out_shape[1] * out_shape[2]), jnp.float32)
    for number, offset in enumerate(tap_offsets()):
        flipped = (2 - offset[0], 2 - offset[1], 2 - offset[2])
        sliced = take_window(padded, flipped, out_shape, 1)
        running = running + lax.dot_general(
            kernel_taps[:, number],
            sliced,
            (((0,), (0,)), ((), ())),
            preferred_element_type=jnp.float32,
        )
    return running.reshape((channels,) + tuple(out_shape))


def kernel_gradient(padded, grad_out, stride):
    outputs = grad_out.shape[0]
    channels = padded.shape[0]
    out_shape = grad_out.shape[1:]
    grad_flat = grad_out.reshape(outputs, -1)
    per_tap = []
    for offset in tap_offsets():
        sliced = take_window(padded, offset, out_shape, stride)
        per_tap.append(
            lax.dot_general(
                grad_flat, sliced, (((1,), (1,)), ((), ())), preferred_element_type=jnp.float32
            )
        )
    return jnp.stack(per_tap, axis=1).reshape(outputs, 27 * channels)


def interior_mask(out_shape):
    along_x = lax.broadcasted_iota(jnp.int32, out_shape, 0)
    along_y = lax.broadcasted_iota(jnp.int32, out_shape, 1)
    along_z = lax.broadcasted_iota(jnp.int32, out_shape, 2)
    keep_cells = (along_x > 0) | (lax.axis_index("gx") > 0)
    keep_cells = keep_cells & ((along_y > 0) | (lax.axis_index("gy") > 0))
    keep_cells = keep_cells & ((along_z > 0) | (lax.axis_index("gz") > 0))
    return keep_cells


def per_device(
    fields,
    grain_ids,
    material_table,
    input_weight,
    kernel_fine,
    kernel_down,
    kernel_bottle,
    cotangent,
):
    grains = material_table.shape[0]
    brick_shape = grain_ids.shape
    onehot = (grain_ids.reshape(1, -1) == lax.broadcasted_iota(jnp.int32, (grains, 1), 0)).astype(
        jnp.bfloat16
    )
    material = jnp.dot(material_table.T, onehot, preferred_element_type=jnp.float32)
    mixture = (
        jnp.dot(
            input_weight, fields.reshape(fields.shape[0], -1), preferred_element_type=jnp.float32
        )
        + material
    )
    embedded = jax.nn.silu(mixture).astype(jnp.bfloat16).reshape((-1,) + tuple(brick_shape))
    rimmed = with_halo(embedded, (("gx", 1), ("gy", 2), ("gz", 3)), 2)
    extended_shape = (brick_shape[0] + 1, brick_shape[1] + 1, brick_shape[2] + 1)
    fine_values = jax.nn.silu(correlate(rimmed, kernel_fine, extended_shape, 1))
    fine_ext = jnp.where(interior_mask(extended_shape)[None], fine_values, 0.0).astype(jnp.bfloat16)
    coarse_shape = (brick_shape[0] // 2, brick_shape[1] // 2, brick_shape[2] // 2)
    pre_down = correlate(fine_ext, kernel_down, coarse_shape, 2)
    coarse = jax.nn.silu(pre_down).astype(jnp.bfloat16)
    voxel_count = (
        coarse_shape[0]
        * lax.axis_size("gx")
        * coarse_shape[1]
        * lax.axis_size("gy")
        * coarse_shape[2]
        * lax.axis_size("gz")
    )
    grad_scale = 1.0 / math.sqrt(voxel_count)
    side_rim = with_halo(coarse, (("gy", 2), ("gz", 3)), 1)
    slab_input = gathered_copies(side_rim, "gx", 1)
    slab_input = jnp.pad(slab_input, ((0, 0), (1, 1), (0, 0), (0, 0)))
    slab_shape = (slab_input.shape[1] - 2, coarse_shape[1], coarse_shape[2])
    pre_slab = correlate(slab_input, kernel_bottle, slab_shape, 1)
    bottle = jax.nn.silu(pre_slab).astype(jnp.bfloat16)
    grad_pre_bottle = (cotangent.astype(jnp.float32) * silu_grad(pre_slab)).astype(jnp.bfloat16)
    grad_padded = with_halo(grad_pre_bottle, (("gy", 2), ("gz", 3)), 1)
    grad_padded = jnp.pad(grad_padded, ((0, 0), (1, 1), (0, 0), (0, 0)))
    partial_act = transpose_correlate(grad_padded, kernel_bottle, slab_shape)
    grad_down_act = sum_at_owner(partial_act.astype(jnp.bfloat16), "gx", 1)
    bottle_part = kernel_gradient(slab_input, grad_pre_bottle, 1) * grad_scale
    grad_pre_down = (grad_down_act * silu_grad(pre_down)).astype(jnp.bfloat16)
    down_part = kernel_gradient(fine_ext, grad_pre_down, 2) * grad_scale
    down_part = sum_at_owner(down_part.astype(jnp.bfloat16), "gx", 0)
    grad_down, grad_bottle = (
        sum_at_owner(down_part.astype(jnp.bfloat16), ("gy", "gz"), 1),
        sum_at_owner(bottle_part.astype(jnp.bfloat16), ("gy", "gz"), 1),
    )
    return (bottle, grad_down, grad_bottle)


def solution(mesh):
    placed = (
        P(None, "gx", "gy", "gz"),
        P("gx", "gy", "gz"),
        P(),
        P(),
        P(),
        P(),
        P("gx", None),
        P("gx", None, "gy", "gz"),
    )
    return jax.shard_map(
        per_device,
        mesh=mesh,
        in_specs=placed,
        out_specs=(P("gx", None, "gy", "gz"), P("gx", ("gy", "gz")), P("gx", ("gy", "gz"))),
        check_vma=False,
    )
```

profile of v0, /device:TPU:1, one launch (start us, length us, event | category | flops | bytes accessed | tf_op | source)
XLA Modules:
  0.0 259.2 jit_solution(18134501945186176915)
XLA Ops:
  3.9 3.9 %collective-permute-start = (bf16[64,2,8,16]{0,3,2,1:T(8,128)(2,1)S(1)}, bf16[64,2,8,16]{0,3,2,1:T(8,128)(2,1)S(1)}, u32[]{:S(2)}, u32[]{:S(2)}) collective-permute-start(bf16[64,2,8,16]{0,3,2,1:T(8,128)(2,1)S(1)} %get-tuple-element.160), channel_id=1, source_target_pairs={{0,32},{32,64},{64,96},{96,128},{128,160},{160,192},{192,224},{1,3... | collective-permute-start | bytes 98312 | tf_op jit(solution)/shard_map/ppermute | solution.py:14
  12.9 4.9 %collective-permute-start.2 = (bf16[64,12,2,16]{0,3,2,1:T(8,128)(2,1)S(1)}, bf16[64,12,2,16]{0,3,2,1:T(8,128)(2,1)S(1)}, u32[]{:S(2)}, u32[]{:S(2)}) collective-permute-start(bf16[64,12,2,16]{0,3,2,1:T(8,128)(2,1)S(1)} %get-tuple-element.127), channel_id=1, source_target_pairs={{0,8},{8,16},{16,24},{1,9},{9,17},{17,25},{2,10},{10,18},{18,26},{... | collective-permute-start | bytes 147464 | tf_op jit(solution)/shard_map/ppermute | solution.py:14
  19.5 6.5 %collective-permute-done.3 = bf16[64,12,2,16]{0,3,2,1:T(8,128)(2,1)S(1)} collective-permute-done((bf16[64,12,2,16]{0,3,2,1:T(8,128)(2,1)S(1)}, bf16[64,12,2,16]{0,3,2,1:T(8,128)(2,1)S(1)}, u32[]{:S(2)}, u32[]{:S(2)}) %collective-permute-start.3) | collective-permute-done | bytes 49184 | tf_op jit(solution)/shard_map/ppermute | solution.py:17
  26.1 7.2 %collective-permute-start.4 = (bf16[64,12,12,2]{0,3,2,1:T(2,128)(2,1)S(1)}, bf16[64,12,12,2]{0,3,2,1:T(2,128)(2,1)S(1)}, u32[]{:S(2)}, u32[]{:S(2)}) collective-permute-start(bf16[64,12,12,2]{0,3,2,1:T(2,128)(2,1)S(1)} %get-tuple-element.65), channel_id=1, source_target_pairs={{0,1},{1,2},{2,3},{3,4},{4,5},{5,6},{6,7},{8,9},{9,10},{10,11},{11... | collective-permute-start | bytes 110600 | tf_op jit(solution)/shard_map/ppermute | solution.py:14
  33.3 2.1 collective-permute-start.5
  36.1 2.9 %collective-permute-done.5 = bf16[64,12,12,2]{0,3,2,1:T(2,128)(2,1)S(1)} collective-permute-done((bf16[64,12,12,2]{0,3,2,1:T(2,128)(2,1)S(1)}, bf16[64,12,12,2]{0,3,2,1:T(2,128)(2,1)S(1)}, u32[]{:S(2)}, u32[]{:S(2)}) %collective-permute-start.5) | collective-permute-done | bytes 36896 | tf_op jit(solution)/shard_map/ppermute | solution.py:17
  39.4 3.5 %fusion.284 = (bf16[64,9,9,17]{0,3,2,1:T(8,128)(2,1)S(1)}, bf16[64,9,9,17]{0,3,2,1:T(8,128)(2,1)}, bf16[64,9,9,17]{0,3,2,1:T(8,128)(2,1)}, bf16[64,9,9,17]{0,3,2...) fusion(bf16[64,12,12,18]{0,3,2,1:T(8,128)(2,1)S(1)} %get-tuple-, ...), kind=kLoop, calls=%fused_computation.530 | loop fusion | bytes 6345216 | tf_op jit(solution)/shard_map/slice | solution.py:71
  46.9 2.1 fusion.285
  49.0 2.0 reshape.443
  53.9 2.0 reshape.446
  57.7 2.0 reshape.449
  65.4 2.0 reshape.455
  67.5 2.0 reshape.456
  107.8 6.8 %collective-permute-start.6 = (bf16[128,4,1,8]{0,3,2,1:T(8,128)(2,1)S(1)}, bf16[128,4,1,8]{0,3,2,1:T(8,128)(2,1)S(1)}, u32[]{:S(2)}, u32[]{:S(2)}) collective-permute-start(bf16[128,4,1,8]{0,3,2,1:T(8,128)(2,1)S(1)} %get-tuple-element.164), channel_id=1, source_target_pairs={{0,8},{8,16},{16,24},{1,9},{9,17},{17,25},{2,10},{10,18},{18,26},{... | collective-permute-start | bytes 24584 | tf_op jit(solution)/shard_map/ppermute | solution.py:14
  115.9 4.0 %collective-permute-done.7 = bf16[128,4,1,8]{0,3,2,1:T(8,128)(2,1)S(1)} collective-permute-done((bf16[128,4,1,8]{0,3,2,1:T(8,128)(2,1)S(1)}, bf16[128,4,1,8]{0,3,2,1:T(8,128)(2,1)S(1)}, u32[]{:S(2)}, u32[]{:S(2)}) %collective-permute-start.7) | collective-permute-done | bytes 8224 | tf_op jit(solution)/shard_map/ppermute | solution.py:17
  120.0 3.3 %collective-permute-start.8 = (bf16[128,4,6,1]{0,3,2,1:T(2,128)(2,1)S(1)}, bf16[128,4,6,1]{0,3,2,1:T(2,128)(2,1)S(1)}, u32[]{:S(2)}, u32[]{:S(2)}) collective-permute-start(bf16[128,4,6,1]{0,3,2,1:T(2,128)(2,1)S(1)} %get-tuple-element.162), channel_id=1, source_target_pairs={{0,1},{1,2},{2,3},{3,4},{4,5},{5,6},{6,7},{8,9},{9,10},{10,11},{11... | collective-permute-start | bytes 18440 | tf_op jit(solution)/shard_map/ppermute | solution.py:14
  125.2 3.1 %collective-permute-done.9 = bf16[128,4,6,1]{0,3,2,1:T(2,128)(2,1)S(1)} collective-permute-done((bf16[128,4,6,1]{0,3,2,1:T(2,128)(2,1)S(1)}, bf16[128,4,6,1]{0,3,2,1:T(2,128)(2,1)S(1)}, u32[]{:S(2)}, u32[]{:S(2)}) %collective-permute-start.9) | collective-permute-done | bytes 6176 | tf_op jit(solution)/shard_map/ppermute | solution.py:17
  129.3 3.9 %all-to-all-start = ((bf16[8,128,4,6,10]{1,2,4,3,0:T(4,128)(2,1)}), bf16[8,128,4,6,10]{1,2,4,3,0:T(4,128)(2,1)S(1)}, u32[]{:S(2)}, u32[]{:S(2)}) async-start(bf16[8,128,4,6,10]{1,2,4,3,0:T(4,128)(2,1)} %broadcast_in_dim.21), calls=%async_computation | async-start | bytes 983040 | tf_op jit(solution)/shard_map/all_to_all | solution.py:30
  134.7 6.7 %all-to-all-done = bf16[8,128,4,6,10]{1,2,4,3,0:T(4,128)(2,1)S(1)} async-done(((bf16[8,128,4,6,10]{1,2,4,3,0:T(4,128)(2,1)}), bf16[8,128,4,6,10]{1,2,4,3,0:T(4,128)(2,1)S(1)}, u32[]{:S(2)}, u32[]{:S(2)}) %all-to-all-start) | async-done | bytes 491552 | tf_op jit(solution)/shard_map/all_to_all | solution.py:30
  160.9 3.1 %collective-permute-start.10 = (bf16[32,32,1,8]{0,3,2,1:T(8,128)(2,1)S(1)}, bf16[32,32,1,8]{0,3,2,1:T(8,128)(2,1)S(1)}, u32[]{:S(2)}, u32[]{:S(2)}) collective-permute-start(bf16[32,32,1,8]{0,3,2,1:T(8,128)(2,1)S(1)} %get-tuple-element.131), channel_id=1, source_target_pairs={{0,8},{8,16},{16,24},{1,9},{9,17},{17,25},{2,10},{10,18},{18,26},{... | collective-permute-start | bytes 49160 | tf_op jit(solution)/shard_map/ppermute | solution.py:14
  165.8 4.6 %collective-permute-done.11 = bf16[32,32,1,8]{0,3,2,1:T(8,128)(2,1)S(1)} collective-permute-done((bf16[32,32,1,8]{0,3,2,1:T(8,128)(2,1)S(1)}, bf16[32,32,1,8]{0,3,2,1:T(8,128)(2,1)S(1)}, u32[]{:S(2)}, u32[]{:S(2)}) %collective-permute-start.11) | collective-permute-done | bytes 16416 | tf_op jit(solution)/shard_map/ppermute | solution.py:17
  170.5 5.0 %collective-permute-start.12 = (bf16[32,32,6,1]{0,3,2,1:T(2,128)(2,1)S(1)}, bf16[32,32,6,1]{0,3,2,1:T(2,128)(2,1)S(1)}, u32[]{:S(2)}, u32[]{:S(2)}) collective-permute-start(bf16[32,32,6,1]{0,3,2,1:T(2,128)(2,1)S(1)} %get-tuple-element.126), channel_id=1, source_target_pairs={{0,1},{1,2},{2,3},{3,4},{4,5},{5,6},{6,7},{8,9},{9,10},{10,11},{11... | collective-permute-start | bytes 36872 | tf_op jit(solution)/shard_map/ppermute | solution.py:14
  175.5 2.1 collective-permute-start.13
  177.7 3.7 %collective-permute-done.13 = bf16[32,32,6,1]{0,3,2,1:T(2,128)(2,1)S(1)} collective-permute-done((bf16[32,32,6,1]{0,3,2,1:T(2,128)(2,1)S(1)}, bf16[32,32,6,1]{0,3,2,1:T(2,128)(2,1)S(1)}, u32[]{:S(2)}, u32[]{:S(2)}) %collective-permute-start.13) | collective-permute-done | bytes 12320 | tf_op jit(solution)/shard_map/ppermute | solution.py:17
  194.5 4.2 %all-to-all-start.1 = ((bf16[8,128,4,4,8]{1,4,3,2,0:T(8,128)(2,1)}), bf16[8,128,4,4,8]{1,4,3,2,0:T(8,128)(2,1)S(1)}, u32[]{:S(2)}, u32[]{:S(2)}) async-start(bf16[8,128,4,4,8]{1,4,3,2,0:T(8,128)(2,1)} %bitcast.160), calls=%async_computation.1 | async-start | bytes 524288 | tf_op jit(solution)/shard_map/all_to_all | solution.py:46
  199.6 5.2 %all-to-all-done.1 = bf16[8,128,4,4,8]{1,4,3,2,0:T(8,128)(2,1)S(1)} async-done(((bf16[8,128,4,4,8]{1,4,3,2,0:T(8,128)(2,1)}), bf16[8,128,4,4,8]{1,4,3,2,0:T(8,128)(2,1)S(1)}, u32[]{:S(2)}, u32[]{:S(2)}) %all-to-all-start.1) | async-done | bytes 262176 | tf_op jit(solution)/shard_map/all_to_all | solution.py:46
  213.6 3.5 %all-to-all-start.2 = ((bf16[8,16,1728]{2,1,0:T(8,128)(2,1)}), bf16[8,16,1728]{2,1,0:T(8,128)(2,1)S(1)}, u32[]{:S(2)}, u32[]{:S(2)}) async-start(bf16[8,16,1728]{2,1,0:T(8,128)(2,1)} %convert_element_type.69), calls=%async_computation.2 | async-start | bytes 917504 | tf_op jit(solution)/shard_map/all_to_all | solution.py:46
  220.4 4.8 %all-to-all-done.2 = bf16[8,16,1728]{2,1,0:T(8,128)(2,1)S(1)} async-done(((bf16[8,16,1728]{2,1,0:T(8,128)(2,1)}), bf16[8,16,1728]{2,1,0:T(8,128)(2,1)S(1)}, u32[]{:S(2)}, u32[]{:S(2)}) %all-to-all-start.2) | async-done | bytes 442400 | tf_op jit(solution)/shard_map/all_to_all | solution.py:46
  225.2 6.0 %all-to-all-start.4 = ((bf16[32,32,108]{2,1,0:T(8,128)(2,1)}), bf16[32,32,108]{2,1,0:T(8,128)(2,1)S(1)}, u32[]{:S(2)}, u32[]{:S(2)}) async-start(bf16[32,32,108]{2,1,0:T(8,128)(2,1)} %copy.233), calls=%async_computation.4 | async-start | bytes 524288 | tf_op jit(solution)/shard_map/all_to_all | solution.py:46
  233.9 11.1 %all-to-all-done.4 = bf16[32,32,108]{2,1,0:T(8,128)(2,1)S(1)} async-done(((bf16[32,32,108]{2,1,0:T(8,128)(2,1)}), bf16[32,32,108]{2,1,0:T(8,128)(2,1)S(1)}, u32[]{:S(2)}, u32[]{:S(2)}) %all-to-all-start.4) | async-done | bytes 221216 | tf_op jit(solution)/shard_map/all_to_all | solution.py:46
  245.0 3.6 %all-to-all-start.3 = ((bf16[32,2,432]{2,1,0:T(2,128)(2,1)}), bf16[32,2,432]{2,1,0:T(2,128)(2,1)S(1)}, u32[]{:S(2)}, u32[]{:S(2)}) async-start(bf16[32,2,432]{2,1,0:T(2,128)(2,1)} %reshape.610), calls=%async_computation.3 | async-start | bytes 131072 | tf_op jit(solution)/shard_map/all_to_all | solution.py:46
  249.3 8.9 %all-to-all-done.3 = bf16[32,2,432]{2,1,0:T(2,128)(2,1)S(1)} async-done(((bf16[32,2,432]{2,1,0:T(2,128)(2,1)}), bf16[32,2,432]{2,1,0:T(2,128)(2,1)S(1)}, u32[]{:S(2)}, u32[]{:S(2)}) %all-to-all-start.3) | async-done | bytes 55328 | tf_op jit(solution)/shard_map/all_to_all | solution.py:46
  (580 shorter events, 118.9 us)
Async XLA Ops:
  3.9 8.0 %collective-permute-start = (bf16[64,2,8,16]{0,3,2,1:T(8,128)(2,1)S(1)}, bf16[64,2,8,16]{0,3,2,1:T(8,128)(2,1)S(1)}, u32[]{:S(2)}, u32[]{:S(2)}) collective-permute-start(bf16[64,2,8,16]{0,3,2,1:T(8,128)(2,1)S(1)} %get-tuple-element.160), channel_id=1, source_target_pairs={{0,32},{32,64},{64,96},{96,128},{128,160},{160,192},{192,224},{1,3... | collective-permute-start | bytes 98312 | tf_op jit(solution)/shard_map/ppermute | solution.py:14
  7.9 5.0 %collective-permute-start.1 = (bf16[64,2,8,16]{0,3,2,1:T(8,128)(2,1)S(1)}, bf16[64,2,8,16]{0,3,2,1:T(8,128)(2,1)S(1)}, u32[]{:S(2)}, u32[]{:S(2)}) collective-permute-start(bf16[64,2,8,16]{0,3,2,1:T(8,128)(2,1)S(1)} %get-tuple-element.161), channel_id=1, source_target_pairs={{32,0},{64,32},{96,64},{128,96},{160,128},{192,160},{224,192},{33,... | collective-permute-start | bytes 98312 | tf_op jit(solution)/shard_map/ppermute | solution.py:17
  12.9 6.5 %collective-permute-start.2 = (bf16[64,12,2,16]{0,3,2,1:T(8,128)(2,1)S(1)}, bf16[64,12,2,16]{0,3,2,1:T(8,128)(2,1)S(1)}, u32[]{:S(2)}, u32[]{:S(2)}) collective-permute-start(bf16[64,12,2,16]{0,3,2,1:T(8,128)(2,1)S(1)} %get-tuple-element.127), channel_id=1, source_target_pairs={{0,8},{8,16},{16,24},{1,9},{9,17},{17,25},{2,10},{10,18},{18,26},{... | collective-permute-start | bytes 147464 | tf_op jit(solution)/shard_map/ppermute | solution.py:14
  17.8 8.1 %collective-permute-start.3 = (bf16[64,12,2,16]{0,3,2,1:T(8,128)(2,1)S(1)}, bf16[64,12,2,16]{0,3,2,1:T(8,128)(2,1)S(1)}, u32[]{:S(2)}, u32[]{:S(2)}) collective-permute-start(bf16[64,12,2,16]{0,3,2,1:T(8,128)(2,1)S(1)} %get-tuple-element.128), channel_id=1, source_target_pairs={{8,0},{16,8},{24,16},{9,1},{17,9},{25,17},{10,2},{18,10},{26,18},{... | collective-permute-start | bytes 147464 | tf_op jit(solution)/shard_map/ppermute | solution.py:17
  26.1 10.0 %collective-permute-start.4 = (bf16[64,12,12,2]{0,3,2,1:T(2,128)(2,1)S(1)}, bf16[64,12,12,2]{0,3,2,1:T(2,128)(2,1)S(1)}, u32[]{:S(2)}, u32[]{:S(2)}) collective-permute-start(bf16[64,12,12,2]{0,3,2,1:T(2,128)(2,1)S(1)} %get-tuple-element.65), channel_id=1, source_target_pairs={{0,1},{1,2},{2,3},{3,4},{4,5},{5,6},{6,7},{8,9},{9,10},{10,11},{11... | collective-permute-start | bytes 110600 | tf_op jit(solution)/shard_map/ppermute | solution.py:14
  33.3 5.7 %collective-permute-start.5 = (bf16[64,12,12,2]{0,3,2,1:T(2,128)(2,1)S(1)}, bf16[64,12,12,2]{0,3,2,1:T(2,128)(2,1)S(1)}, u32[]{:S(2)}, u32[]{:S(2)}) collective-permute-start(bf16[64,12,12,2]{0,3,2,1:T(2,128)(2,1)S(1)} %get-tuple-element.66), channel_id=1, source_target_pairs={{1,0},{2,1},{3,2},{4,3},{5,4},{6,5},{7,6},{9,8},{10,9},{11,10},{12... | collective-permute-start | bytes 110600 | tf_op jit(solution)/shard_map/ppermute | solution.py:17
  107.7 25.5 %copy-start.57 = (bf16[32,3456]{1,0:T(8,128)(2,1)S(1)}, bf16[32,3456]{1,0:T(8,128)(2,1)}, u32[]{:S(2)}) copy-start(bf16[32,3456]{1,0:T(8,128)(2,1)} %param.14) | copy-start | bytes 663556
  107.8 8.1 %collective-permute-start.6 = (bf16[128,4,1,8]{0,3,2,1:T(8,128)(2,1)S(1)}, bf16[128,4,1,8]{0,3,2,1:T(8,128)(2,1)S(1)}, u32[]{:S(2)}, u32[]{:S(2)}) collective-permute-start(bf16[128,4,1,8]{0,3,2,1:T(8,128)(2,1)S(1)} %get-tuple-element.164), channel_id=1, source_target_pairs={{0,8},{8,16},{16,24},{1,9},{9,17},{17,25},{2,10},{10,18},{18,26},{... | collective-permute-start | bytes 24584 | tf_op jit(solution)/shard_map/ppermute | solution.py:14
  114.6 5.4 %collective-permute-start.7 = (bf16[128,4,1,8]{0,3,2,1:T(8,128)(2,1)S(1)}, bf16[128,4,1,8]{0,3,2,1:T(8,128)(2,1)S(1)}, u32[]{:S(2)}, u32[]{:S(2)}) collective-permute-start(bf16[128,4,1,8]{0,3,2,1:T(8,128)(2,1)S(1)} %get-tuple-element.165), channel_id=1, source_target_pairs={{8,0},{16,8},{24,16},{9,1},{17,9},{25,17},{10,2},{18,10},{26,18},{... | collective-permute-start | bytes 24584 | tf_op jit(solution)/shard_map/ppermute | solution.py:17
  120.0 5.2 %collective-permute-start.8 = (bf16[128,4,6,1]{0,3,2,1:T(2,128)(2,1)S(1)}, bf16[128,4,6,1]{0,3,2,1:T(2,128)(2,1)S(1)}, u32[]{:S(2)}, u32[]{:S(2)}) collective-permute-start(bf16[128,4,6,1]{0,3,2,1:T(2,128)(2,1)S(1)} %get-tuple-element.162), channel_id=1, source_target_pairs={{0,1},{1,2},{2,3},{3,4},{4,5},{5,6},{6,7},{8,9},{9,10},{10,11},{11... | collective-permute-start | bytes 18440 | tf_op jit(solution)/shard_map/ppermute | solution.py:14
  123.3 5.0 %collective-permute-start.9 = (bf16[128,4,6,1]{0,3,2,1:T(2,128)(2,1)S(1)}, bf16[128,4,6,1]{0,3,2,1:T(2,128)(2,1)S(1)}, u32[]{:S(2)}, u32[]{:S(2)}) collective-permute-start(bf16[128,4,6,1]{0,3,2,1:T(2,128)(2,1)S(1)} %get-tuple-element.163), channel_id=1, source_target_pairs={{1,0},{2,1},{3,2},{4,3},{5,4},{6,5},{7,6},{9,8},{10,9},{11,10},{12... | collective-permute-start | bytes 18440 | tf_op jit(solution)/shard_map/ppermute | solution.py:17
  129.3 12.1 %all-to-all-start = ((bf16[8,128,4,6,10]{1,2,4,3,0:T(4,128)(2,1)}), bf16[8,128,4,6,10]{1,2,4,3,0:T(4,128)(2,1)S(1)}, u32[]{:S(2)}, u32[]{:S(2)}) async-start(bf16[8,128,4,6,10]{1,2,4,3,0:T(4,128)(2,1)} %broadcast_in_dim.21), calls=%async_computation | async-start | bytes 983040 | tf_op jit(solution)/shard_map/all_to_all | solution.py:30
  134.2 14.7 %copy-start.103 = (bf16[32,1,128]{2,1,0:T(2,128)(2,1)}, bf16[32,1,128]{2,1,0:T(2,128)(2,1)S(1)}, u32[]{:S(2)}) copy-start(bf16[32,1,128]{2,1,0:T(2,128)(2,1)S(1)} %get-tuple-element.154) | copy-start | bytes 24580
  134.2 14.9 %copy-start.101 = (bf16[32,1,128]{2,1,0:T(2,128)(2,1)}, bf16[32,1,128]{2,1,0:T(2,128)(2,1)S(1)}, u32[]{:S(2)}) copy-start(bf16[32,1,128]{2,1,0:T(2,128)(2,1)S(1)} %get-tuple-element.153) | copy-start | bytes 24580
  134.2 15.1 %copy-start.99 = (bf16[32,1,128]{2,1,0:T(2,128)(2,1)}, bf16[32,1,128]{2,1,0:T(2,128)(2,1)S(1)}, u32[]{:S(2)}) copy-start(bf16[32,1,128]{2,1,0:T(2,128)(2,1)S(1)} %get-tuple-element.152) | copy-start | bytes 24580
  134.6 14.9 %copy-start.97 = (bf16[32,1,128]{2,1,0:T(2,128)(2,1)}, bf16[32,1,128]{2,1,0:T(2,128)(2,1)S(1)}, u32[]{:S(2)}) copy-start(bf16[32,1,128]{2,1,0:T(2,128)(2,1)S(1)} %get-tuple-element.151) | copy-start | bytes 24580
  134.6 15.1 %copy-start.95 = (bf16[32,1,128]{2,1,0:T(2,128)(2,1)}, bf16[32,1,128]{2,1,0:T(2,128)(2,1)S(1)}, u32[]{:S(2)}) copy-start(bf16[32,1,128]{2,1,0:T(2,128)(2,1)S(1)} %get-tuple-element.150) | copy-start | bytes 24580
  134.6 15.3 %copy-start.93 = (bf16[32,1,128]{2,1,0:T(2,128)(2,1)}, bf16[32,1,128]{2,1,0:T(2,128)(2,1)S(1)}, u32[]{:S(2)}) copy-start(bf16[32,1,128]{2,1,0:T(2,128)(2,1)S(1)} %get-tuple-element.149) | copy-start | bytes 24580
  134.6 15.5 %copy-start.113 = (bf16[32,1,128]{2,1,0:T(2,128)(2,1)}, bf16[32,1,128]{2,1,0:T(2,128)(2,1)S(1)}, u32[]{:S(2)}) copy-start(bf16[32,1,128]{2,1,0:T(2,128)(2,1)S(1)} %get-tuple-element.148) | copy-start | bytes 24580
  134.7 15.7 %copy-start.91 = (bf16[32,1,128]{2,1,0:T(2,128)(2,1)}, bf16[32,1,128]{2,1,0:T(2,128)(2,1)S(1)}, u32[]{:S(2)}) copy-start(bf16[32,1,128]{2,1,0:T(2,128)(2,1)S(1)} %get-tuple-element.147) | copy-start | bytes 24580
  134.7 15.9 %copy-start.89 = (bf16[32,1,128]{2,1,0:T(2,128)(2,1)}, bf16[32,1,128]{2,1,0:T(2,128)(2,1)S(1)}, u32[]{:S(2)}) copy-start(bf16[32,1,128]{2,1,0:T(2,128)(2,1)S(1)} %get-tuple-element.146) | copy-start | bytes 24580
  134.7 16.1 %copy-start.87 = (bf16[32,1,128]{2,1,0:T(2,128)(2,1)}, bf16[32,1,128]{2,1,0:T(2,128)(2,1)S(1)}, u32[]{:S(2)}) copy-start(bf16[32,1,128]{2,1,0:T(2,128)(2,1)S(1)} %get-tuple-element.145) | copy-start | bytes 24580
  134.7 16.3 %copy-start.85 = (bf16[32,1,128]{2,1,0:T(2,128)(2,1)}, bf16[32,1,128]{2,1,0:T(2,128)(2,1)S(1)}, u32[]{:S(2)}) copy-start(bf16[32,1,128]{2,1,0:T(2,128)(2,1)S(1)} %get-tuple-element.144) | copy-start | bytes 24580
  160.9 4.8 %collective-permute-start.10 = (bf16[32,32,1,8]{0,3,2,1:T(8,128)(2,1)S(1)}, bf16[32,32,1,8]{0,3,2,1:T(8,128)(2,1)S(1)}, u32[]{:S(2)}, u32[]{:S(2)}) collective-permute-start(bf16[32,32,1,8]{0,3,2,1:T(8,128)(2,1)S(1)} %get-tuple-element.131), channel_id=1, source_target_pairs={{0,8},{8,16},{16,24},{1,9},{9,17},{17,25},{2,10},{10,18},{18,26},{... | collective-permute-start | bytes 49160 | tf_op jit(solution)/shard_map/ppermute | solution.py:14
  164.1 6.3 %collective-permute-start.11 = (bf16[32,32,1,8]{0,3,2,1:T(8,128)(2,1)S(1)}, bf16[32,32,1,8]{0,3,2,1:T(8,128)(2,1)S(1)}, u32[]{:S(2)}, u32[]{:S(2)}) collective-permute-start(bf16[32,32,1,8]{0,3,2,1:T(8,128)(2,1)S(1)} %get-tuple-element.132), channel_id=1, source_target_pairs={{8,0},{16,8},{24,16},{9,1},{17,9},{25,17},{10,2},{18,10},{26,18},{... | collective-permute-start | bytes 49160 | tf_op jit(solution)/shard_map/ppermute | solution.py:17
  170.5 7.2 %collective-permute-start.12 = (bf16[32,32,6,1]{0,3,2,1:T(2,128)(2,1)S(1)}, bf16[32,32,6,1]{0,3,2,1:T(2,128)(2,1)S(1)}, u32[]{:S(2)}, u32[]{:S(2)}) collective-permute-start(bf16[32,32,6,1]{0,3,2,1:T(2,128)(2,1)S(1)} %get-tuple-element.126), channel_id=1, source_target_pairs={{0,1},{1,2},{2,3},{3,4},{4,5},{5,6},{6,7},{8,9},{9,10},{10,11},{11... | collective-permute-start | bytes 36872 | tf_op jit(solution)/shard_map/ppermute | solution.py:14
  175.5 5.9 %collective-permute-start.13 = (bf16[32,32,6,1]{0,3,2,1:T(2,128)(2,1)S(1)}, bf16[32,32,6,1]{0,3,2,1:T(2,128)(2,1)S(1)}, u32[]{:S(2)}, u32[]{:S(2)}) collective-permute-start(bf16[32,32,6,1]{0,3,2,1:T(2,128)(2,1)S(1)} %get-tuple-element.125), channel_id=1, source_target_pairs={{1,0},{2,1},{3,2},{4,3},{5,4},{6,5},{7,6},{9,8},{10,9},{11,10},{12... | collective-permute-start | bytes 36872 | tf_op jit(solution)/shard_map/ppermute | solution.py:17
  194.5 10.3 %all-to-all-start.1 = ((bf16[8,128,4,4,8]{1,4,3,2,0:T(8,128)(2,1)}), bf16[8,128,4,4,8]{1,4,3,2,0:T(8,128)(2,1)S(1)}, u32[]{:S(2)}, u32[]{:S(2)}) async-start(bf16[8,128,4,4,8]{1,4,3,2,0:T(8,128)(2,1)} %bitcast.160), calls=%async_computation.1 | async-start | bytes 524288 | tf_op jit(solution)/shard_map/all_to_all | solution.py:46
  213.6 11.7 %all-to-all-start.2 = ((bf16[8,16,1728]{2,1,0:T(8,128)(2,1)}), bf16[8,16,1728]{2,1,0:T(8,128)(2,1)S(1)}, u32[]{:S(2)}, u32[]{:S(2)}) async-start(bf16[8,16,1728]{2,1,0:T(8,128)(2,1)} %convert_element_type.69), calls=%async_computation.2 | async-start | bytes 917504 | tf_op jit(solution)/shard_map/all_to_all | solution.py:46
  225.2 19.7 %all-to-all-start.4 = ((bf16[32,32,108]{2,1,0:T(8,128)(2,1)}), bf16[32,32,108]{2,1,0:T(8,128)(2,1)S(1)}, u32[]{:S(2)}, u32[]{:S(2)}) async-start(bf16[32,32,108]{2,1,0:T(8,128)(2,1)} %copy.233), calls=%async_computation.4 | async-start | bytes 524288 | tf_op jit(solution)/shard_map/all_to_all | solution.py:46
  231.3 27.8 %copy-start.1 = (bf16[128,64]{0,1:T(8,128)(2,1)S(1)}, bf16[128,64]{0,1:T(8,128)(2,1)}, u32[]{:S(2)}) copy-start(bf16[128,64]{0,1:T(8,128)(2,1)} %param.10) | copy-start | bytes 49156
  245.0 13.2 %all-to-all-start.3 = ((bf16[32,2,432]{2,1,0:T(2,128)(2,1)}), bf16[32,2,432]{2,1,0:T(2,128)(2,1)S(1)}, u32[]{:S(2)}, u32[]{:S(2)}) async-start(bf16[32,2,432]{2,1,0:T(2,128)(2,1)} %reshape.610), calls=%async_computation.3 | async-start | bytes 131072 | tf_op jit(solution)/shard_map/all_to_all | solution.py:46
  (122 other events, 481.8 us)
where the time goes:
time: 264 us; the launch traced here: 259 us
  local copies, waits for them, and re-layouts  81.4 us (31%)
  starting transfers between devices  66.7 us (25%)
  waiting for transfers between devices  62.9 us (24%)
  matrix products  39.8 us (15%)
  other arithmetic  5.05 us (2%)
  between operations  3.37 us (1%)
    ppermute x7, starting transfers between devices, with_halo(): lax.ppermute(lax.slice_in_dim(block, block.shape[dim] - width, None, axis...  34.2 us
    reshape x27, local copies, waits for them, and re-layouts, take_window(): return sliced.reshape(padded.shape[0], -1)  30.6 us
    all_to_all x4, waiting for transfers between devices, sum_at_owner(): lax.all_to_all(pieces, axis, split_axis=0, concat_axis=0, tiled=True)  30.1 us
    ppermute x7, waiting for transfers between devices, with_halo(): lax.ppermute(lax.slice_in_dim(block, 0, width, axis=dim), axis, backward)  25.8 us
    slice x61, local copies, waits for them, and re-layouts, take_window(): lax.slice(padded, (0, offset[0], offset[1], offset[2]), limits, (1, strid...  24.5 us
    all_to_all x4, starting transfers between devices, sum_at_owner(): lax.all_to_all(pieces, axis, split_axis=0, concat_axis=0, tiled=True)  17.3 us
    dot_general x81, matrix products, correlate(): jnp.dot(kernel_taps[:, number], sliced, preferred_element_type=jnp.float32)  16.6 us
    dot_general x54, matrix products, kernel_gradient(): lax.dot_general(grad_flat, sliced, (((1,), (1,)), ((), ())), preferred_el...  16.1 us
  transfers between devices with their start and end apart: 19, of which 13 were waited for; matrix products, arithmetic and copies ran while one was open for 5% of the time, Pallas kernels for 0%

commit v1 on v0

v1 whole, which is shorter than its diff:
```python
import functools
import math

import jax
import jax.numpy as jnp
from jax import lax
from jax.experimental import pallas as pl
from jax.experimental.pallas import tpu as pltpu
from jax.sharding import PartitionSpec as P

MESH = pl.DeviceIdType.MESH
F32 = jnp.float32
BF16 = jnp.bfloat16
NT = (((1,), (1,)), ((), ()))


def silu(v):
    return v * jax.nn.sigmoid(v)


def silu_grad(v):
    s = jax.nn.sigmoid(v)
    return s * (1.0 + v * (1.0 - s))


def dot(a, b):
    return jnp.dot(a, b, preferred_element_type=F32)


def dot_nt(a, b):
    return lax.dot_general(a, b, NT, preferred_element_type=F32)


def tap_of(t):
    t = min(t, 26)
    return t // 9, (t // 3) % 3, t % 3


def lane_iota(shape):
    return lax.broadcasted_iota(jnp.int32, shape, len(shape) - 1)


def piece(ref_tiles, start, width):
    tile, shift = start // 128, start % 128
    low = ref_tiles(tile)
    if shift == 0:
        return low
    low = pltpu.roll(low, 128 - shift, 1)
    if shift + width <= 128:
        return low
    high = pltpu.roll(ref_tiles(tile + 1), 128 - shift, 1)
    return jnp.where(lane_iota(low.shape) < 128 - shift, low, high)


def body(
    sizes,
    fields,
    ids,
    table,
    w_in,
    k_fine,
    k_down,
    k_bot,
    cot,
    bottle_o,
    gdown_o,
    gbot_o,
    raw,
    brick,
    ext,
    es,
    af,
    fs,
    fmask,
    kf,
    kd,
    kb4,
    wblk,
    ac,
    ad,
    pd,
    cb,
    cs,
    sb,
    slab,
    a3,
    pre,
    gp,
    gt,
    ysend,
    zsend,
    csend,
    yrecv,
    zrecv,
    crecv,
    gpad,
    ag,
    acts,
    actr,
    downs,
    downr,
    dsum,
    gball,
    gbs,
    gbr,
    gds,
    gdr,
    sem_l,
    s1,
    r1,
    s2,
    r2,
    s3,
    r3,
    s4,
    r4,
    s5,
    r5,
    s6,
    r6,
    s7,
    r7,
):
    nx, ny, nz = sizes
    gx, gy, gz = lax.axis_index("gx"), lax.axis_index("gy"), lax.axis_index("gz")
    scale = 1.0 / math.sqrt(nx * 4 * ny * 4 * nz * 8)

    def device(dx, dy, dz):
        return (lax.rem(gx + dx + nx, nx), lax.rem(gy + dy + ny, ny), lax.rem(gz + dz + nz, nz))

    near = [(dx, dy, dz) for dx in (-1, 0, 1) for dy in (-1, 0, 1) for dz in (-1, 0, 1)]
    near = [n for n in near if n != (0, 0, 0)]
    columns = [(dx, 0, 0) for dx in range(1, nx)]
    planes = [(0, dy, dz) for dy in range(ny) for dz in range(nz) if (dy, dz) != (0, 0)]
    partners = sorted({(a % nx, b % ny, c % nz) for a, b, c in near + columns + planes})
    barrier = pltpu.get_barrier_semaphore()
    for p in partners:
        pl.semaphore_signal(barrier, inc=1, device_id=device(*p), device_id_type=MESH)

    sel_row = lax.broadcasted_iota(jnp.int32, (16, 128), 0)
    sel_lane = lax.broadcasted_iota(jnp.int32, (16, 128), 1)
    packed = jnp.zeros((64, 128), F32)
    for ch in range(8):
        plane = (fields[ch] if ch < 7 else ids[...]).astype(F32).reshape(64, 16).astype(BF16)
        select = jnp.where(sel_lane == sel_row * 8 + ch, 1.0, 0.0).astype(BF16)
        packed = packed + dot(plane, select)
    raw[...] = packed
    group = lane_iota((16, 128)) // 32
    for zb in range(4):
        block = None
        for y4 in range(4):
            rows = raw[pl.ds(y4, 16, stride=4), :]
            shift = ((y4 - zb) * 32) % 128
            rows = rows if shift == 0 else pltpu.roll(rows, shift, 1)
            block = rows if block is None else jnp.where(group == y4, rows, block)
        for r in range(16):
            brick[r // 2, r % 2, zb, :, :] = block[r : r + 1, :]
    ext[:, :, 6:8] = jnp.zeros((11, 4, 2, 1, 128), F32)

    kf[...] = jnp.zeros(kf.shape, BF16)
    kf[0:64, 0:1728] = k_fine[...]
    kf[64:128, 0:1728] = k_fine[...]
    kd[...] = jnp.zeros(kd.shape, BF16)
    kd[:, 0:1728] = k_down[...]
    for q in range(4):
        kb4[32 * q : 32 * q + 32, :] = k_bot[...]
    wblk[...] = jnp.zeros(wblk.shape, BF16)
    for t in range(27):
        for q in range(4):
            wblk[t * 128 + q * 32 : t * 128 + q * 32 + 32, q * 128 : q * 128 + 128] = k_bot[
                :, t * 128 : t * 128 + 128
            ]
    my = gy * 8 - 3 + lax.broadcasted_iota(jnp.int32, (13, 24, 128), 0)
    mz = gz * 16 - 3 + lax.broadcasted_iota(jnp.int32, (13, 24, 128), 1)
    inside = (my >= 0) & (my < ny * 8) & (mz >= 0) & (mz < nz * 16)
    fmask[...] = jnp.where(inside, 1.0, 0.0)
    fs[...] = jnp.zeros(fs.shape, F32)
    gpad[...] = jnp.zeros(gpad.shape, F32)
    slab[0] = jnp.zeros((64, 128), F32)
    slab[4 * nx + 1] = jnp.zeros((64, 128), F32)
    cb[...] = jnp.zeros(cb.shape, F32)

    pl.semaphore_wait(barrier, len(partners))

    x_src = {1: (6, 2, 0), 0: (0, 8, 2), -1: (0, 1, 10)}
    y_src = {1: (1, 1, 0), 0: (0, 2, 1), -1: (0, 1, 3)}
    z_src = {1: (3, 1, 0), 0: (0, 4, 1), -1: (0, 1, 5)}
    halo = []
    for number, (dx, dy, dz) in enumerate(near):
        (xs, xn, xd), (ys, yn, yd), (zs, zn, zd) = x_src[dx], y_src[dy], z_src[dz]
        halo.append(
            pltpu.make_async_remote_copy(
                src_ref=brick.at[xs : xs + xn, ys : ys + yn, zs : zs + zn],
                dst_ref=ext.at[xd : xd + xn, yd : yd + yn, zd : zd + zn],
                send_sem=s1.at[number],
                recv_sem=r1.at[number],
                device_id=device(dx, dy, dz),
                device_id_type=MESH,
            )
        )
    for c in halo:
        c.start()
    own = pltpu.make_async_copy(brick, ext.at[2:10, 1:3, 1:5], sem_l.at[0])
    own.start()

    row8 = lax.broadcasted_iota(jnp.int32, (128, 7), 0) % 8
    pick = jnp.where(row8 == lax.broadcasted_iota(jnp.int32, (128, 7), 1), 1.0, 0.0).astype(BF16)
    w_twice = jnp.concatenate([w_in[...].astype(F32)] * 2, axis=0).astype(BF16)
    w_rows = dot_nt(pick, w_twice)
    id_rows = jnp.where(lax.broadcasted_iota(jnp.int32, (128, 128), 0) % 8 == 7, 1.0, 0.0)
    w_emb = jnp.concatenate([id_rows, w_rows], axis=1)
    emb_row = lax.broadcasted_iota(jnp.int32, (128, 256), 0) // 8
    twice = jnp.where(
        lax.broadcasted_iota(jnp.int32, (64, 128), 1) % 64
        == lax.broadcasted_iota(jnp.int32, (64, 128), 0),
        1.0,
        0.0,
    ).astype(BF16)
    table2 = dot(table[...], twice).astype(BF16)

    own.wait()
    for c in halo:
        c.wait()

    blocks = ext[...].reshape(44, 8, 128)
    bx = lax.broadcasted_iota(jnp.int32, (44, 8, 128), 0)
    by = bx % 4
    bx = bx // 4
    bz = lax.broadcasted_iota(jnp.int32, (44, 8, 128), 1)
    outside = ((bx < 2) & (gx == 0)) | ((bx == 10) & (gx == nx - 1))
    outside = outside | ((by == 0) & (gy == 0)) | ((by == 3) & (gy == ny - 1))
    outside = outside | ((bz == 0) & (gz == 0)) | ((bz == 5) & (gz == nz - 1))
    fill = jnp.where(lane_iota((44, 8, 128)) % 8 == 7, -1.0, 0.0)
    blocks = jnp.where(outside, fill, blocks).reshape(352, 128).astype(BF16)
    lanes = lane_iota((352, 128)).astype(F32)
    for p in range(16):
        y4, z4 = p // 4, p % 4
        w_p = jnp.where(emb_row == p, w_emb, 0.0).astype(BF16)
        both = dot(blocks, w_p)
        onehot = jnp.where(both[:, 0:128] == lanes, 1.0, 0.0).astype(BF16)
        value = silu(both[:, 128:256] + dot(onehot, table2)).reshape(11, 4, 8, 128)
        for x in range(11):
            for yb in range(4):
                es[x, yb * 4 + y4, pl.ds(z4, 8, stride=4), :] = value[x, yb]

    half = lane_iota((13, 24, 128)) < 64

    def fine_plane(x, carry):
        for t in range(14):
            (ax, ay, az), (bx_, by_, bz_) = tap_of(2 * t), tap_of(2 * t + 1)
            low = es[x + ax, ay : ay + 13, az : az + 24, :]
            high = es[x + bx_, by_ : by_ + 13, bz_ : bz_ + 24, :]
            block = jnp.where(half, low, high)
            af[:, t * 128 : t * 128 + 128] = block.reshape(312, 128).astype(BF16)
        value = silu(dot_nt(af[...], kf[...])).reshape(13, 24, 128)
        keep = jnp.where((x > 0) | (gx > 0), 1.0, 0.0)
        value = value * fmask[...] * keep
        fs[x, :, 0:24, :] = value.astype(BF16).astype(F32)
        return carry

    lax.fori_loop(0, 9, fine_plane, 0)

    half16 = lane_iota((16, 128)) < 64
    for x in range(4):
        for y in range(6):
            row = (x * 6 + y) * 16
            for t in range(14):
                (ax, ay, az), (bx_, by_, bz_) = tap_of(2 * t), tap_of(2 * t + 1)
                low = fs[2 * x + ax, 2 * y + ay, pl.ds(az, 16, stride=2), :]
                high = fs[2 * x + bx_, 2 * y + by_, pl.ds(bz_, 16, stride=2), :]
                ac[row : row + 16, t * 128 : t * 128 + 128] = jnp.where(half16, low, high).astype(BF16)
    pd[...] = dot_nt(ac[...], kd[...]).reshape(4, 6, 16, 128)
    coarse = silu(pd[...])
    cy = gy * 4 - 1 + lax.broadcasted_iota(jnp.int32, (4, 6, 16, 128), 1)
    cz = gz * 8 - 1 + lax.broadcasted_iota(jnp.int32, (4, 6, 16, 128), 2)
    inside = (cy >= 0) & (cy < ny * 4) & (cz >= 0) & (cz < nz * 8)
    coarse = jnp.where(inside, coarse, 0.0)
    for x in range(4):
        for y in range(6):
            cb[x, y * 10 : y * 10 + 10, :] = coarse[x, y, 0:10, :]
    cs[...] = cb[...].astype(BF16)

    gather = []
    for k in range(1, nx):
        gather.append(
            pltpu.make_async_remote_copy(
                src_ref=cs,
                dst_ref=sb.at[gx],
                send_sem=s2.at[k],
                recv_sem=r2.at[k],
                device_id=device(k, 0, 0),
                device_id_type=MESH,
            )
        )
    for c in gather:
        c.start()

    half8 = lane_iota((8, 128)) < 64
    for y in range(4):
        for t in range(14):
            (ax, ay, az), (bx_, by_, bz_) = tap_of(2 * t), tap_of(2 * t + 1)
            parts = []
            for x in range(4):
                low = fs[2 * x + ax, 2 * y + 2 + ay, pl.ds(2 + az, 8, stride=2), :]
                high = fs[2 * x + bx_, 2 * y + 2 + by_, pl.ds(2 + bz_, 8, stride=2), :]
                parts.append(jnp.where(half8, low, high))
            ad[y * 32 : y * 32 + 32, t * 128 : t * 128 + 128] = jnp.concatenate(parts, axis=0).astype(BF16)

    slab[pl.ds(1 + gx * 4, 4)] = cs[...].astype(F32)
    for k, c in enumerate(gather, 1):
        c.wait()
        source = lax.rem(gx - k + nx, nx)
        slab[pl.ds(1 + source * 4, 4)] = sb[source].astype(F32)

    for y in range(4):
        for t in range(27):
            ax, ay, az = tap_of(t)
            start = (y + ay) * 10 + az
            window = slab[ax : ax + 32, start : start + 8, :].reshape(4, 64, 128).astype(BF16)
            a3[:, y * 64 : y * 64 + 64, t * 128 : t * 128 + 128] = window

    def bottle_group(q, carry):
        pre[q] = dot_nt(a3[q], kb4[...])
        return carry

    lax.fori_loop(0, 4, bottle_group, 0)
    group = lane_iota((256, 128)) // 32
    z = pre[0]
    for q in range(1, 4):
        z = jnp.where(group == q, pre[q], z)
    bottle_o[...] = silu(z).reshape(4, 64, 128).astype(BF16)
    grad = cot[...].astype(F32).reshape(256, 128) * silu_grad(z)
    grad = grad.astype(BF16).astype(F32)
    gp[...] = grad.reshape(4, 64, 128)

    for side in range(2):
        ysend[side] = gp[3 - 3 * side].astype(BF16)
        zsend[side] = jnp.concatenate(
            [gp[y, pl.ds(7 - 7 * side, 8, stride=8), :] for y in range(4)], axis=0
        ).astype(BF16)
        for other in range(2):
            corner = gp[3 - 3 * side, pl.ds(7 - 7 * other, 8, stride=8), :]
            csend[side * 2 + other] = jnp.concatenate([corner, corner], axis=0).astype(BF16)
    rim = []

    def rim_copy(src, dst, number, dy, dz):
        c = pltpu.make_async_remote_copy(
            src_ref=src,
            dst_ref=dst,
            send_sem=s3.at[number],
            recv_sem=r3.at[number],
            device_id=device(0, dy, dz),
            device_id_type=MESH,
        )
        c.start()
        rim.append(c)

    for side in range(2):
        rim_copy(ysend.at[side], yrecv.at[side], side, 1 - 2 * side, 0)
    for side in range(2):
        rim_copy(zsend.at[side], zrecv.at[side], 2 + side, 0, 1 - 2 * side)
    for corner in range(4):
        rim_copy(
            csend.at[corner],
            crecv.at[corner],
            4 + corner,
            1 - 2 * (corner // 2),
            1 - 2 * (corner % 2),
        )

    gt[...] = jnp.transpose(grad).astype(BF16)
    for n in range(9):
        total = None
        for q in range(4):
            part = dot(gt[32 * q : 32 * q + 32, :], a3[q, :, n * 384 : n * 384 + 384])
            total = part if total is None else total + part
        gball[:, n * 384 : n * 384 + 384] = total * scale
    for k in range(ny * nz):
        cut = piece(lambda tile: gball[:, tile * 128 : tile * 128 + 128], 108 * k, 108)
        gbs[k] = cut.astype(BF16)
    me = gy * nz + gz
    gb_copies = []
    for k, (_, dy, dz) in enumerate(planes):
        ty, tz = lax.rem(gy + dy, ny), lax.rem(gz + dz, nz)
        gb_copies.append(
            pltpu.make_async_remote_copy(
                src_ref=gbs.at[ty * nz + tz],
                dst_ref=gbr.at[me],
                send_sem=s6.at[k],
                recv_sem=r6.at[k],
                device_id=(gx, ty, tz),
                device_id_type=MESH,
            )
        )

    gpad[1:5, 1:9, 1:9, :] = gp[...].reshape(4, 8, 8, 128)
    for c in rim:
        c.wait()
    for c in gb_copies:
        c.start()

    def kept(flag, value):
        return jnp.where(flag, value.astype(F32), 0.0)

    y_ok = (gy > 0, gy < ny - 1)
    z_ok = (gz > 0, gz < nz - 1)
    for side in range(2):
        gpad[5 * side, 1:9, 1:9, :] = kept(y_ok[side], yrecv[side]).reshape(8, 8, 128)
        value = kept(z_ok[side], zrecv[side])
        for y in range(4):
            gpad[1 + y, 1:9, 9 * side : 9 * side + 1, :] = value[8 * y : 8 * y + 8].reshape(8, 1, 128)
        for other in range(2):
            value = kept(y_ok[side] & z_ok[other], crecv[side * 2 + other])
            gpad[5 * side, 1:9, 9 * other : 9 * other + 1, :] = value[0:8].reshape(8, 1, 128)
    edge = lane_iota((96, 128))
    low = pltpu.roll(gpad[:, 8, :, :].reshape(96, 128), 32, 1)
    gpad[:, 0, :, :] = jnp.where(edge < 32, 0.0, low).reshape(6, 16, 128)
    high = pltpu.roll(gpad[:, 1, :, :].reshape(96, 128), 96, 1)
    gpad[:, 9, :, :] = jnp.where(edge >= 96, 0.0, high).reshape(6, 16, 128)

    for t in range(27):
        ax, ay, az = tap_of(t)
        window = gpad[2 - ay : 6 - ay, 2 - ax : 10 - ax, 2 - az : 10 - az, :]
        ag[:, t * 128 : t * 128 + 128] = window.reshape(256, 128).astype(BF16)
    for q in range(4):
        act = dot(ag[...], wblk[:, q * 128 : q * 128 + 128]).reshape(4, 64, 128).astype(BF16)
        for part in range(2):
            acts[2 * q + part] = act[:, part * 32 : part * 32 + 32, :]
    act_copies = []
    for k in range(1, nx):
        target = lax.rem(gx + k, nx)
        act_copies.append(
            pltpu.make_async_remote_copy(
                src_ref=acts.at[target],
                dst_ref=actr.at[gx],
                send_sem=s4.at[k],
                recv_sem=r4.at[k],
                device_id=(target, gy, gz),
                device_id_type=MESH,
            )
        )
    for c in act_copies:
        c.start()
    slope = []
    for y in range(4):
        for x in range(4):
            slope.append(silu_grad(pd[x, y + 1, 1:9, :]))
    slope = jnp.concatenate(slope, axis=0)
    total = acts[gx].astype(F32)
    for k, c in enumerate(act_copies, 1):
        c.wait()
        total = total + actr[lax.rem(gx - k + nx, nx)].astype(F32)
    grad_down = (total.reshape(128, 128) * slope).astype(BF16).astype(F32)
    grad_down_t = jnp.transpose(grad_down).astype(BF16)

    part = dot(grad_down_t, ad[...]) * scale
    downs[...] = part.reshape(nx, 16, 1792).astype(BF16)
    down_copies = []
    for k in range(1, nx):
        target = lax.rem(gx + k, nx)
        down_copies.append(
            pltpu.make_async_remote_copy(
                src_ref=downs.at[target],
                dst_ref=downr.at[gx],
                send_sem=s5.at[k],
                recv_sem=r5.at[k],
                device_id=(target, gy, gz),
                device_id_type=MESH,
            )
        )
    for c in down_copies:
        c.start()

    total = gbs[me].astype(F32)
    for k, c in enumerate(gb_copies):
        c.wait()
    for k, (_, dy, dz) in enumerate(planes):
        source = lax.rem(gy - dy + ny, ny) * nz + lax.rem(gz - dz + nz, nz)
        total = total + gbr[source].astype(F32)
    gbot_o[...] = total[:, 0:108]

    dsum[...] = downs[gx].astype(F32)
    for k, c in enumerate(down_copies, 1):
        c.wait()
        dsum[...] += downr[lax.rem(gx - k + nx, nx)].astype(F32)
    for k in range(ny * nz):
        cut = piece(lambda tile: dsum[:, tile * 128 : tile * 128 + 128], 54 * k, 54)
        gds[k] = cut.astype(BF16)
    gd_copies = []
    for k, (_, dy, dz) in enumerate(planes):
        ty, tz = lax.rem(gy + dy, ny), lax.rem(gz + dz, nz)
        c = pltpu.make_async_remote_copy(
            src_ref=gds.at[ty * nz + tz],
            dst_ref=gdr.at[me],
            send_sem=s7.at[k],
            recv_sem=r7.at[k],
            device_id=(gx, ty, tz),
            device_id_type=MESH,
        )
        c.start()
        gd_copies.append(c)
    total = gds[me].astype(F32)
    for c in gd_copies:
        c.wait()
    for k, (_, dy, dz) in enumerate(planes):
        source = lax.rem(gy - dy + ny, ny) * nz + lax.rem(gz - dz + nz, nz)
        total = total + gdr[source].astype(F32)
    gdown_o[...] = total[:, 0:54]


def per_device(sizes, fields, grain_ids, table, w_in, k_fine, k_down, k_bot, cotangent):
    nx, ny, nz = sizes
    n = ny * nz
    cot = cotangent.reshape(32, 4, 8, 4, 8).transpose(3, 2, 4, 1, 0).reshape(4, 64, 128)
    vmem = pl.BlockSpec(memory_space=pltpu.VMEM)
    V = pltpu.VMEM
    D = pltpu.SemaphoreType.DMA
    scratch = [
        V((64, 128), F32),
        V((8, 2, 4, 1, 128), F32),
        V((11, 4, 8, 1, 128), F32),
        V((11, 16, 32, 128), F32),
        V((312, 1792), BF16),
        V((9, 13, 40, 128), F32),
        V((13, 24, 128), F32),
        V((128, 1792), BF16),
        V((128, 1792), BF16),
        V((128, 3456), BF16),
        V((3456, 512), BF16),
        V((384, 1792), BF16),
        V((128, 1792), BF16),
        V((4, 6, 16, 128), F32),
        V((4, 64, 128), F32),
        V((4, 64, 128), BF16),
        V((nx, 4, 64, 128), BF16),
        V((4 * nx + 2, 64, 128), F32),
        V((4, 256, 3456), BF16),
        V((4, 256, 128), F32),
        V((4, 64, 128), F32),
        V((128, 256), BF16),
        V((2, 64, 128), BF16),
        V((2, 32, 128), BF16),
        V((4, 16, 128), BF16),
        V((2, 64, 128), BF16),
        V((2, 32, 128), BF16),
        V((4, 16, 128), BF16),
        V((6, 10, 16, 128), F32),
        V((256, 3456), BF16),
        V((nx, 4, 32, 128), BF16),
        V((nx, 4, 32, 128), BF16),
        V((nx, 16, 1792), BF16),
        V((nx, 16, 1792), BF16),
        V((16, 1792), F32),
        V((32, 3456), F32),
        V((n, 32, 128), BF16),
        V((n, 32, 128), BF16),
        V((n, 16, 128), BF16),
        V((n, 16, 128), BF16),
        D((1,)),
        D((26,)),
        D((26,)),
        D((nx,)),
        D((nx,)),
        D((8,)),
        D((8,)),
        D((nx,)),
        D((nx,)),
        D((nx,)),
        D((nx,)),
        D((n,)),
        D((n,)),
        D((n,)),
        D((n,)),
    ]
    bottle, grad_down, grad_bottle = pl.pallas_call(
        functools.partial(body, sizes),
        out_shape=(
            jax.ShapeDtypeStruct((4, 64, 128), BF16),
            jax.ShapeDtypeStruct((16, 54), F32),
            jax.ShapeDtypeStruct((32, 108), F32),
        ),
        in_specs=[vmem] * 8,
        out_specs=(vmem, vmem, vmem),
        scratch_shapes=scratch,
        compiler_params=pltpu.CompilerParams(
            collective_id=0, has_side_effects=True, vmem_limit_bytes=60 * 1024 * 1024
        ),
    )(fields, grain_ids, table, w_in, k_fine, k_down, k_bot, cot)
    bottle = bottle.reshape(4, 8, 8, 4, 32).transpose(4, 3, 1, 0, 2).reshape(32, 32, 4, 8)
    return bottle, grad_down, grad_bottle


def solution(mesh):
    sizes = (mesh.shape["gx"], mesh.shape["gy"], mesh.shape["gz"])
    placed = (
        P(None, "gx", "gy", "gz"),
        P("gx", "gy", "gz"),
        P(),
        P(),
        P(),
        P(),
        P("gx", None),
        P("gx", None, "gy", "gz"),
    )
    return jax.shard_map(
        functools.partial(per_device, sizes),
        mesh=mesh,
        in_specs=placed,
        out_specs=(P("gx", None, "gy", "gz"), P("gx", ("gy", "gz")), P("gx", ("gy", "gz"))),
        check_vma=False,
    )
```

time: 264 us -> 82.7 us (0.31); the launches traced: 259 us -> 82.4 us
  Pallas kernels: 0 us -> 72.5 us
  local copies, waits for them, and re-layouts: 81.4 us -> 9.21 us
  starting transfers between devices: 66.7 us -> 0 us
  waiting for transfers between devices: 62.9 us -> 0 us
  matrix products: 39.8 us -> 0 us
  other arithmetic: 5.05 us -> 0 us
  between operations: 3.37 us -> 0.7 us
    pallas_call x0 -> x1, Pallas kernels: none -> 72.5 us  [per_device(): pl.pallas_call(functools.partial(body, sizes), out_shape=(jax.ShapeDtypeS...]
    ppermute x14 -> x0, starting transfers between devices: 45.5 us -> none  [the longest x7 34.2 us: with_halo(): lax.ppermute(lax.slice_in_dim(block, block.shape[dim] - width, None, axis...]
    dot_general x164 -> x0, matrix products: 39.8 us -> none  [the longest x81 16.6 us: correlate(): jnp.dot(kernel_taps[:, number], sliced, preferred_element_type=jnp.float32)]
    all_to_all x5 -> x0, waiting for transfers between devices: 36.8 us -> none  [the longest x4 30.1 us: sum_at_owner(): lax.all_to_all(pieces, axis, split_axis=0, concat_axis=0, tiled=True)]
    reshape x32 -> x3, local copies, waits for them, and re-layouts: 32.8 us -> 1.83 us  [the longest x2 1.03 us: per_device(): bottle.reshape(4, 8, 8, 4, 32).transpose(4, 3, 1, 0, 2)]
    slice x68 -> x0, local copies, waits for them, and re-layouts: 27.2 us -> none  [the longest x61 24.5 us: take_window(): lax.slice(padded, (0, offset[0], offset[1], offset[2]), limits, (1, strid...]
    ppermute x14 -> x0, waiting for transfers between devices: 26.1 us -> none  [the longest x7 25.8 us: with_halo(): lax.ppermute(lax.slice_in_dim(block, 0, width, axis=dim), axis, backward)]
    all_to_all x5 -> x0, starting transfers between devices: 21.2 us -> none  [the longest x4 17.3 us: sum_at_owner(): lax.all_to_all(pieces, axis, split_axis=0, concat_axis=0, tiled=True)]
  transfers between devices with their start and end apart: 19 -> 0, of which waited for: 13 -> 0; matrix products, arithmetic and copies ran while one was open for 5% -> 0% of each run, Pallas kernels for 0% -> 0%
where the time goes in v1:
time: 82.7 us; the launch traced here: 82.4 us
  Pallas kernels  72.5 us (88%)
  local copies, waits for them, and re-layouts  9.21 us (11%)
    pallas_call x1, Pallas kernels, per_device(): pl.pallas_call(functools.partial(body, sizes), out_shape=(jax.ShapeDtypeS...  72.5 us
    unnamed x15, local copies, waits for them, and re-layouts  7.17 us

profile of v1, /device:TPU:1, one launch (start us, length us, event | category | flops | bytes accessed | tf_op | source)
XLA Modules:
  0.0 82.4 jit_solution(11059642877959792981)
XLA Ops:
  0.6 0.0 copy-start.1
  0.6 1.4 %copy.19.w_in = bf16[64,7]{1,0:T(8,128)(2,1)} copy(bf16[64,7]{0,1:T(8,128)(2,1)} %param.11) | data formatting | bytes 1792 | tf_op args[3]
  2.0 0.0 copy-done.1
  2.0 0.7 copy.18.table
  2.8 1.5 %copy.16 = bf16[32,32,4,8]{0,3,2,1:T(8,128)(2,1)S(1)} copy(bf16[32,32,4,8]{1,3,2,0:T(8,128)(2,1)} %param.15) | data formatting | bytes 131072 | tf_op args[7]
  4.3 0.0 copy-start
  4.3 0.2 copy.17
  4.5 0.8 reshape.19.cot
  5.3 0.0 copy-done
  5.3 1.0 %copy.20.k_down = bf16[128,1728]{1,0:T(8,128)(2,1)} copy(bf16[128,1728]{0,1:T(8,128)(2,1)S(1)} %copy-done) | data formatting | bytes 884736 | tf_op args[5]
  6.3 72.5 %shard_map.103 = (bf16[4,64,128]{2,1,0:T(8,128)(2,1)}, f32[16,54]{1,0:T(8,128)}, f32[32,108]{1,0:T(8,128)}) custom-call(bf16[7,8,8,16]{3,2,1,0:T(8,128)(2,1)} %fields.1, s32[8,8,16]{2,1,0:T(8,128)} %ids.1, bf16[128,64]{1,0:T(8,128)(2,1)} %copy.18.table, bf16[64,7]{1,0:T(8,128)(2,1)} %copy.19.w_in, bf16[64,1728]{1,0:T(8,128)(2,1)} %k_fine.1, ...), custom_call_target="tpu_custom_call" | custom-call | tf_op jit(solution)/shard_map/pallas_call | solution.py:575
  78.8 1.0 %reshape.20 = bf16[4,8,8,4,32]{4,3,2,1,0:T(4,128)(2,1)S(1)} reshape(bf16[4,64,128]{2,1,0:T(8,128)(2,1)} %get-tuple-element.6) | data formatting | bytes 131072 | tf_op jit(solution)/shard_map/reshape | solution.py:589
  79.8 0.0 copy-start.3
  79.8 1.2 %copy.22 = bf16[32,32,4,8]{1,3,2,0:T(8,128)(2,1)} copy(bf16[32,32,4,8]{0,3,2,1:T(8,128)(2,1)S(1)} %bitcast.6) | data formatting | bytes 131072
  81.0 0.0 copy-done.3
  81.0 0.0 copy-start.2
  81.0 0.6 copy.25
  81.6 0.1 copy-done.2
  81.8 0.6 copy.26
  (1 shorter events, 0.0 us)
Async XLA Ops:
  0.6 1.4 %copy-start.1 = (bf16[128,64]{0,1:T(8,128)(2,1)S(1)}, bf16[128,64]{0,1:T(8,128)(2,1)}, u32[]{:S(2)}) copy-start(bf16[128,64]{0,1:T(8,128)(2,1)} %param.10) | copy-start | bytes 49156
  4.3 1.0 %copy-start = (bf16[128,1728]{0,1:T(8,128)(2,1)S(1)}, bf16[128,1728]{0,1:T(8,128)(2,1)}, u32[]{:S(2)}) copy-start(bf16[128,1728]{0,1:T(8,128)(2,1)} %param.13) | copy-start | bytes 1327108
  79.8 1.2 %copy-start.3 = (f32[16,54]{1,0:T(8,128)S(1)}, f32[16,54]{1,0:T(8,128)}, u32[]{:S(2)}) copy-start(f32[16,54]{1,0:T(8,128)} %get-tuple-element.16) | copy-start | bytes 10372
  81.0 0.7 copy-start.2

commit v2 on v1

--- a/solution.py
+++ b/solution.py
@@ -54,17 +54,27 @@
 
 def body(
     sizes,
+    fields_h,
+    ids_h,
+    table_h,
+    w_in_h,
+    k_fine_h,
+    k_down_h,
+    k_bot_h,
+    cot_h,
+    bottle_o,
+    gdown_o,
+    gbot_o,
     fields,
     ids,
     table,
     w_in,
     k_fine,
-    k_down,
-    k_bot,
     cot,
-    bottle_o,
-    gdown_o,
-    gbot_o,
+    cotf,
+    cotp,
+    tt,
+    bo,
     raw,
     brick,
     ext,
@@ -103,6 +113,8 @@
     gball,
     gbs,
     gbr,
+    gb2s,
+    gb2r,
     gds,
     gdr,
     sem_l,
@@ -120,6 +132,8 @@
     r6,
     s7,
     r7,
+    s8,
+    r8,
 ):
     nx, ny, nz = sizes
     gx, gy, gz = lax.axis_index("gx"), lax.axis_index("gy"), lax.axis_index("gz")
@@ -136,6 +150,29 @@
     barrier = pltpu.get_barrier_semaphore()
     for p in partners:
         pl.semaphore_signal(barrier, inc=1, device_id=device(*p), device_id_type=MESH)
+
+    loads = [
+        pltpu.make_async_copy(src, dst, sem_l.at[1 + i])
+        for i, (src, dst) in enumerate(
+            [(fields_h, fields), (ids_h, ids), (table_h, table), (w_in_h, w_in), (k_fine_h, k_fine)]
+            + [(k_down_h, kd.at[0:1728]), (cot_h, cot)]
+            + [(k_bot_h, kb4.at[32 * q : 32 * q + 32]) for q in range(4)]
+        )
+    ]
+    for c in loads:
+        c.start()
+    kd[1728:1792, :] = jnp.zeros((64, 128), BF16)
+    kf[...] = jnp.zeros(kf.shape, BF16)
+    wblk[...] = jnp.zeros(wblk.shape, BF16)
+    fs[...] = jnp.zeros(fs.shape, F32)
+    gpad[...] = jnp.zeros(gpad.shape, F32)
+    slab[0] = jnp.zeros((64, 128), F32)
+    slab[4 * nx + 1] = jnp.zeros((64, 128), F32)
+    cb[...] = jnp.zeros(cb.shape, F32)
+    cotf[...] = jnp.zeros(cotf.shape, F32)
+    ext[:, :, 6:8] = jnp.zeros((11, 4, 2, 1, 128), F32)
+    for c in loads[0:2]:
+        c.wait()
 
     sel_row = lax.broadcasted_iota(jnp.int32, (16, 128), 0)
     sel_lane = lax.broadcasted_iota(jnp.int32, (16, 128), 1)
@@ -155,30 +192,20 @@
             block = rows if block is None else jnp.where(group == y4, rows, block)
         for r in range(16):
             brick[r // 2, r % 2, zb, :, :] = block[r : r + 1, :]
-    ext[:, :, 6:8] = jnp.zeros((11, 4, 2, 1, 128), F32)
-
-    kf[...] = jnp.zeros(kf.shape, BF16)
+
+    for c in loads[2:]:
+        c.wait()
     kf[0:64, 0:1728] = k_fine[...]
     kf[64:128, 0:1728] = k_fine[...]
-    kd[...] = jnp.zeros(kd.shape, BF16)
-    kd[:, 0:1728] = k_down[...]
-    for q in range(4):
-        kb4[32 * q : 32 * q + 32, :] = k_bot[...]
-    wblk[...] = jnp.zeros(wblk.shape, BF16)
     for t in range(27):
         for q in range(4):
-            wblk[t * 128 + q * 32 : t * 128 + q * 32 + 32, q * 128 : q * 128 + 128] = k_bot[
-                :, t * 128 : t * 128 + 128
+            wblk[t * 128 + q * 32 : t * 128 + q * 32 + 32, q * 128 : q * 128 + 128] = kb4[
+                0:32, t * 128 : t * 128 + 128
             ]
     my = gy * 8 - 3 + lax.broadcasted_iota(jnp.int32, (13, 24, 128), 0)
     mz = gz * 16 - 3 + lax.broadcasted_iota(jnp.int32, (13, 24, 128), 1)
     inside = (my >= 0) & (my < ny * 8) & (mz >= 0) & (mz < nz * 16)
     fmask[...] = jnp.where(inside, 1.0, 0.0)
-    fs[...] = jnp.zeros(fs.shape, F32)
-    gpad[...] = jnp.zeros(gpad.shape, F32)
-    slab[0] = jnp.zeros((64, 128), F32)
-    slab[4 * nx + 1] = jnp.zeros((64, 128), F32)
-    cb[...] = jnp.zeros(cb.shape, F32)
 
     pl.semaphore_wait(barrier, len(partners))
 
@@ -205,10 +232,6 @@
 
     row8 = lax.broadcasted_iota(jnp.int32, (128, 7), 0) % 8
     pick = jnp.where(row8 == lax.broadcasted_iota(jnp.int32, (128, 7), 1), 1.0, 0.0).astype(BF16)
-    w_twice = jnp.concatenate([w_in[...].astype(F32)] * 2, axis=0).astype(BF16)
-    w_rows = dot_nt(pick, w_twice)
-    id_rows = jnp.where(lax.broadcasted_iota(jnp.int32, (128, 128), 0) % 8 == 7, 1.0, 0.0)
-    w_emb = jnp.concatenate([id_rows, w_rows], axis=1)
     emb_row = lax.broadcasted_iota(jnp.int32, (128, 256), 0) // 8
     twice = jnp.where(
         lax.broadcasted_iota(jnp.int32, (64, 128), 1) % 64
@@ -216,7 +239,10 @@
         1.0,
         0.0,
     ).astype(BF16)
-    table2 = dot(table[...], twice).astype(BF16)
+    w_rows = dot(pick, dot(w_in[...], twice).astype(BF16))
+    table2 = jnp.concatenate([table[...]] * 2, axis=0)
+    id_rows = jnp.where(lax.broadcasted_iota(jnp.int32, (128, 128), 0) % 8 == 7, 1.0, 0.0)
+    w_emb = jnp.concatenate([id_rows, w_rows], axis=1)
 
     own.wait()
     for c in halo:
@@ -238,7 +264,7 @@
         w_p = jnp.where(emb_row == p, w_emb, 0.0).astype(BF16)
         both = dot(blocks, w_p)
         onehot = jnp.where(both[:, 0:128] == lanes, 1.0, 0.0).astype(BF16)
-        value = silu(both[:, 128:256] + dot(onehot, table2)).reshape(11, 4, 8, 128)
+        value = silu(both[:, 128:256] + dot_nt(onehot, table2)).reshape(11, 4, 8, 128)
         for x in range(11):
             for yb in range(4):
                 es[x, yb * 4 + y4, pl.ds(z4, 8, stride=4), :] = value[x, yb]
@@ -258,42 +284,42 @@
         fs[x, :, 0:24, :] = value.astype(BF16).astype(F32)
         return carry
 
-    lax.fori_loop(0, 9, fine_plane, 0)
+    def coarse_copy(x, k):
+        return pltpu.make_async_remote_copy(
+            src_ref=cs.at[x],
+            dst_ref=sb.at[gx, x],
+            send_sem=s2.at[x, k],
+            recv_sem=r2.at[x, k],
+            device_id=device(k, 0, 0),
+            device_id_type=MESH,
+        )
 
     half16 = lane_iota((16, 128)) < 64
-    for x in range(4):
+    cy = gy * 4 - 1 + lax.broadcasted_iota(jnp.int32, (6, 16, 128), 0)
+    cz = gz * 8 - 1 + lax.broadcasted_iota(jnp.int32, (6, 16, 128), 1)
+    inside = (cy >= 0) & (cy < ny * 4) & (cz >= 0) & (cz < nz * 8)
+
+    def coarse_plane(x, carry):
+        lax.fori_loop(2 * x + 1, 2 * x + 3, fine_plane, 0)
         for y in range(6):
-            row = (x * 6 + y) * 16
+            row = y * 16
             for t in range(14):
                 (ax, ay, az), (bx_, by_, bz_) = tap_of(2 * t), tap_of(2 * t + 1)
                 low = fs[2 * x + ax, 2 * y + ay, pl.ds(az, 16, stride=2), :]
                 high = fs[2 * x + bx_, 2 * y + by_, pl.ds(bz_, 16, stride=2), :]
                 ac[row : row + 16, t * 128 : t * 128 + 128] = jnp.where(half16, low, high).astype(BF16)
-    pd[...] = dot_nt(ac[...], kd[...]).reshape(4, 6, 16, 128)
-    coarse = silu(pd[...])
-    cy = gy * 4 - 1 + lax.broadcasted_iota(jnp.int32, (4, 6, 16, 128), 1)
-    cz = gz * 8 - 1 + lax.broadcasted_iota(jnp.int32, (4, 6, 16, 128), 2)
-    inside = (cy >= 0) & (cy < ny * 4) & (cz >= 0) & (cz < nz * 8)
-    coarse = jnp.where(inside, coarse, 0.0)
-    for x in range(4):
+        before = dot(ac[...], kd[...]).reshape(6, 16, 128)
+        pd[x] = before
+        coarse = jnp.where(inside, silu(before), 0.0)
         for y in range(6):
-            cb[x, y * 10 : y * 10 + 10, :] = coarse[x, y, 0:10, :]
-    cs[...] = cb[...].astype(BF16)
-
-    gather = []
-    for k in range(1, nx):
-        gather.append(
-            pltpu.make_async_remote_copy(
-                src_ref=cs,
-                dst_ref=sb.at[gx],
-                send_sem=s2.at[k],
-                recv_sem=r2.at[k],
-                device_id=device(k, 0, 0),
-                device_id_type=MESH,
-            )
-        )
-    for c in gather:
-        c.start()
+            cb[x, y * 10 : y * 10 + 10, :] = coarse[y, 0:10, :]
+        cs[x] = cb[x].astype(BF16)
+        for k in range(1, nx):
+            coarse_copy(x, k).start()
+        return carry
+
+    fine_plane(0, 0)
+    lax.fori_loop(0, 4, coarse_plane, 0)
 
     half8 = lane_iota((8, 128)) < 64
     for y in range(4):
@@ -307,8 +333,20 @@
             ad[y * 32 : y * 32 + 32, t * 128 : t * 128 + 128] = jnp.concatenate(parts, axis=0).astype(BF16)
 
     slab[pl.ds(1 + gx * 4, 4)] = cs[...].astype(F32)
-    for k, c in enumerate(gather, 1):
-        c.wait()
+
+    cotf[:, 0:32] = cot[...].astype(F32).reshape(1024, 32)
+    group = lane_iota((32, 128)) // 8
+    spread = lax.broadcasted_iota(jnp.int32, (8, 128), 0)
+    spread = jnp.where(lane_iota((8, 128)) % 8 == spread, 1.0, 0.0).astype(BF16)
+    for y in range(4):
+        for z in range(8):
+            rows = cotf[pl.ds(y * 8 + z, 32, stride=32), :]
+            rows = jnp.concatenate([jnp.where(group == q, rows, 0.0) for q in range(4)], axis=0)
+            cotp[y, pl.ds(z, 8, stride=8), :] = dot_nt(spread, rows.astype(BF16))
+
+    for k in range(1, nx):
+        for x in range(4):
+            coarse_copy(x, k).wait()
         source = lax.rem(gx - k + nx, nx)
         slab[pl.ds(1 + source * 4, 4)] = sb[source].astype(F32)
 
@@ -328,8 +366,7 @@
     z = pre[0]
     for q in range(1, 4):
         z = jnp.where(group == q, pre[q], z)
-    bottle_o[...] = silu(z).reshape(4, 64, 128).astype(BF16)
-    grad = cot[...].astype(F32).reshape(256, 128) * silu_grad(z)
+    grad = cotp[...].reshape(256, 128) * silu_grad(z)
     grad = grad.astype(BF16).astype(F32)
     gp[...] = grad.reshape(4, 64, 128)
 
@@ -377,18 +414,18 @@
         gball[:, n * 384 : n * 384 + 384] = total * scale
     for k in range(ny * nz):
         cut = piece(lambda tile: gball[:, tile * 128 : tile * 128 + 128], 108 * k, 108)
-        gbs[k] = cut.astype(BF16)
+        gbs[k % nz, k // nz] = cut.astype(BF16)
     me = gy * nz + gz
     gb_copies = []
-    for k, (_, dy, dz) in enumerate(planes):
-        ty, tz = lax.rem(gy + dy, ny), lax.rem(gz + dz, nz)
+    for k in range(1, nz):
+        target = lax.rem(gz + k, nz)
         gb_copies.append(
             pltpu.make_async_remote_copy(
-                src_ref=gbs.at[ty * nz + tz],
-                dst_ref=gbr.at[me],
+                src_ref=gbs.at[target],
+                dst_ref=gbr.at[gz],
                 send_sem=s6.at[k],
                 recv_sem=r6.at[k],
-                device_id=(gx, ty, tz),
+                device_id=(gx, gy, target),
                 device_id_type=MESH,
             )
         )
@@ -422,34 +459,55 @@
         ax, ay, az = tap_of(t)
         window = gpad[2 - ay : 6 - ay, 2 - ax : 10 - ax, 2 - az : 10 - az, :]
         ag[:, t * 128 : t * 128 + 128] = window.reshape(256, 128).astype(BF16)
+    def act_copy(slot, target, source):
+        return pltpu.make_async_remote_copy(
+            src_ref=acts.at[target],
+            dst_ref=actr.at[slot],
+            send_sem=s4.at[target],
+            recv_sem=r4.at[source],
+            device_id=(target, gy, gz),
+            device_id_type=MESH,
+        )
+
     for q in range(4):
         act = dot(ag[...], wblk[:, q * 128 : q * 128 + 128]).reshape(4, 64, 128).astype(BF16)
         for part in range(2):
-            acts[2 * q + part] = act[:, part * 32 : part * 32 + 32, :]
-    act_copies = []
-    for k in range(1, nx):
-        target = lax.rem(gx + k, nx)
-        act_copies.append(
-            pltpu.make_async_remote_copy(
-                src_ref=acts.at[target],
-                dst_ref=actr.at[gx],
-                send_sem=s4.at[k],
-                recv_sem=r4.at[k],
-                device_id=(target, gy, gz),
-                device_id_type=MESH,
-            )
-        )
-    for c in act_copies:
-        c.start()
+            target = 2 * q + part
+            acts[target] = act[:, part * 32 : part * 32 + 32, :]
+
+            @pl.when(gx != target)
+            def _(target=target):
+                act_copy(gx, target, gx).start()
+
+    z = pre[0]
+    group = lane_iota((256, 128)) // 32
+    for q in range(1, 4):
+        z = jnp.where(group == q, pre[q], z)
+    out = silu(z).astype(BF16).astype(F32).reshape(4, 64, 128)
+    for y in range(4):
+        turned = jnp.transpose(jnp.concatenate([out[y], jnp.zeros((64, 128), F32)], axis=0))
+        for q in range(4):
+            tt[y * 32 : y * 32 + 32, q * 128 : q * 128 + 128] = turned[q * 32 : q * 32 + 32].astype(BF16)
+    row = lax.broadcasted_iota(jnp.int32, (512, 128), 0)
+    x_of = (row // 128) * 8 + (row % 128) // 8
+    x_of = jnp.where(row % 128 < 64, x_of, -1)
+    for k in range(8):
+        select = jnp.where((x_of == lane_iota((512, 128))) & (row % 8 == k), 1.0, 0.0).astype(BF16)
+        turned = dot(tt[...], select)
+        for y in range(4):
+            bo[pl.ds(y * 8 + k, 32, stride=32), :] = turned[y * 32 : y * 32 + 32]
+    bottle_o[...] = bo[...].reshape(32, 4, 8, 128)[:, :, :, 0:32].astype(BF16)
+
     slope = []
     for y in range(4):
         for x in range(4):
             slope.append(silu_grad(pd[x, y + 1, 1:9, :]))
     slope = jnp.concatenate(slope, axis=0)
     total = acts[gx].astype(F32)
-    for k, c in enumerate(act_copies, 1):
-        c.wait()
-        total = total + actr[lax.rem(gx - k + nx, nx)].astype(F32)
+    for k in range(1, nx):
+        source = lax.rem(gx - k + nx, nx)
+        act_copy(source, lax.rem(gx + k, nx), source).wait()
+        total = total + actr[source].astype(F32)
     grad_down = (total.reshape(128, 128) * slope).astype(BF16).astype(F32)
     grad_down_t = jnp.transpose(grad_down).astype(BF16)
 
@@ -471,22 +529,36 @@
     for c in down_copies:
         c.start()
 
-    total = gbs[me].astype(F32)
-    for k, c in enumerate(gb_copies):
+    total = gbs[gz].astype(F32)
+    for k, c in enumerate(gb_copies, 1):
         c.wait()
-    for k, (_, dy, dz) in enumerate(planes):
-        source = lax.rem(gy - dy + ny, ny) * nz + lax.rem(gz - dz + nz, nz)
-        total = total + gbr[source].astype(F32)
-    gbot_o[...] = total[:, 0:108]
+        total = total + gbr[lax.rem(gz - k + nz, nz)].astype(F32)
+    gb2s[...] = total.astype(BF16)
+    gb2_copies = []
+    for k in range(1, ny):
+        target = lax.rem(gy + k, ny)
+        c = pltpu.make_async_remote_copy(
+            src_ref=gb2s.at[target],
+            dst_ref=gb2r.at[gy],
+            send_sem=s8.at[k],
+            recv_sem=r8.at[k],
+            device_id=(gx, target, gz),
+            device_id_type=MESH,
+        )
+        c.start()
+        gb2_copies.append(c)
 
     dsum[...] = downs[gx].astype(F32)
     for k, c in enumerate(down_copies, 1):
         c.wait()
         dsum[...] += downr[lax.rem(gx - k + nx, nx)].astype(F32)
+    low_half = lane_iota((8, 128)) < 64
     for k in range(ny * nz):
         cut = piece(lambda tile: dsum[:, tile * 128 : tile * 128 + 128], 54 * k, 54)
+        cut = jnp.where(low_half, cut[0:8], pltpu.roll(cut[8:16], 64, 1))
         gds[k] = cut.astype(BF16)
     gd_copies = []
+    planes.sort(key=lambda p: -2 * min(p[1], ny - p[1]) - min(p[2], nz - p[2]))
     for k, (_, dy, dz) in enumerate(planes):
         ty, tz = lax.rem(gy + dy, ny), lax.rem(gz + dz, nz)
         c = pltpu.make_async_remote_copy(
@@ -499,23 +571,39 @@
         )
         c.start()
         gd_copies.append(c)
+    total = gb2s[gy].astype(F32)
+    for k, c in enumerate(gb2_copies, 1):
+        c.wait()
+        total = total + gb2r[lax.rem(gy - k + ny, ny)].astype(F32)
+    gbot_o[...] = total[:, 0:108]
     total = gds[me].astype(F32)
     for c in gd_copies:
         c.wait()
     for k, (_, dy, dz) in enumerate(planes):
         source = lax.rem(gy - dy + ny, ny) * nz + lax.rem(gz - dz + nz, nz)
         total = total + gdr[source].astype(F32)
-    gdown_o[...] = total[:, 0:54]
+    gdown_o[0:8, :] = total[:, 0:54]
+    gdown_o[8:16, :] = pltpu.roll(total, 64, 1)[:, 0:54]
 
 
 def per_device(sizes, fields, grain_ids, table, w_in, k_fine, k_down, k_bot, cotangent):
     nx, ny, nz = sizes
     n = ny * nz
-    cot = cotangent.reshape(32, 4, 8, 4, 8).transpose(3, 2, 4, 1, 0).reshape(4, 64, 128)
+    cot = cotangent.transpose(0, 2, 3, 1)
     vmem = pl.BlockSpec(memory_space=pltpu.VMEM)
     V = pltpu.VMEM
     D = pltpu.SemaphoreType.DMA
     scratch = [
+        V((7, 8, 8, 16), BF16),
+        V((8, 8, 16), jnp.int32),
+        V((64, 128), BF16),
+        V((7, 64), BF16),
+        V((64, 1728), BF16),
+        V((32, 4, 8, 32), BF16),
+        V((1024, 128), F32),
+        V((4, 64, 128), F32),
+        V((128, 512), BF16),
+        V((1024, 128), F32),
         V((64, 128), F32),
         V((8, 2, 4, 1, 128), F32),
         V((11, 4, 8, 1, 128), F32),
@@ -524,10 +612,10 @@
         V((9, 13, 40, 128), F32),
         V((13, 24, 128), F32),
         V((128, 1792), BF16),
-        V((128, 1792), BF16),
+        V((1792, 128), BF16),
         V((128, 3456), BF16),
         V((3456, 512), BF16),
-        V((384, 1792), BF16),
+        V((96, 1792), BF16),
         V((128, 1792), BF16),
         V((4, 6, 16, 128), F32),
         V((4, 64, 128), F32),
@@ -552,42 +640,45 @@
         V((nx, 16, 1792), BF16),
         V((16, 1792), F32),
         V((32, 3456), F32),
-        V((n, 32, 128), BF16),
-        V((n, 32, 128), BF16),
-        V((n, 16, 128), BF16),
-        V((n, 16, 128), BF16),
-        D((1,)),
+        V((nz, ny, 32, 128), BF16),
+        V((nz, ny, 32, 128), BF16),
+        V((ny, 32, 128), BF16),
+        V((ny, 32, 128), BF16),
+        V((n, 8, 128), BF16),
+        V((n, 8, 128), BF16),
+        D((12,)),
         D((26,)),
         D((26,)),
-        D((nx,)),
-        D((nx,)),
+        D((4, nx)),
+        D((4, nx)),
         D((8,)),
         D((8,)),
         D((nx,)),
         D((nx,)),
         D((nx,)),
         D((nx,)),
+        D((nz,)),
+        D((nz,)),
         D((n,)),
         D((n,)),
-        D((n,)),
-        D((n,)),
+        D((ny,)),
+        D((ny,)),
     ]
     bottle, grad_down, grad_bottle = pl.pallas_call(
         functools.partial(body, sizes),
         out_shape=(
-            jax.ShapeDtypeStruct((4, 64, 128), BF16),
+            jax.ShapeDtypeStruct((32, 4, 8, 32), BF16),
             jax.ShapeDtypeStruct((16, 54), F32),
             jax.ShapeDtypeStruct((32, 108), F32),
         ),
-        in_specs=[vmem] * 8,
+        in_specs=[pl.BlockSpec(memory_space=pl.ANY)] * 8,
         out_specs=(vmem, vmem, vmem),
         scratch_shapes=scratch,
         compiler_params=pltpu.CompilerParams(
             collective_id=0, has_side_effects=True, vmem_limit_bytes=60 * 1024 * 1024
         ),
-    )(fields, grain_ids, table, w_in, k_fine, k_down, k_bot, cot)
-    bottle = bottle.reshape(4, 8, 8, 4, 32).transpose(4, 3, 1, 0, 2).reshape(32, 32, 4, 8)
-    return bottle, grad_down, grad_bottle
+    )(fields, grain_ids, table.T, w_in.T, k_fine, k_down.T, k_bot, cot)
+    return bottle.transpose(0, 3, 1, 2), grad_down, grad_bottle
 
 
 def solution(mesh):

time: 82.7 us -> 67.1 us (0.81)
  Pallas kernels: 72.5 us -> 63.2 us
  local copies, waits for them, and re-layouts: 9.21 us -> 3.01 us
    pallas_call x1, Pallas kernels: 72.5 us -> 63.2 us  [per_device(): pl.pallas_call(functools.partial(body, sizes), out_shape=(jax.ShapeDtypeS...]
    unnamed x15 -> x7, local copies, waits for them, and re-layouts: 7.17 us -> 3.01 us
    reshape x3 -> x0, local copies, waits for them, and re-layouts: 1.83 us -> none  [the longest x2 1.03 us: per_device(): bottle.reshape(4, 8, 8, 4, 32).transpose(4, 3, 1, 0, 2)]
where the time goes in v2:
time: 67.1 us; the launch traced here: 66.9 us
  Pallas kernels  63.2 us (94%)
  local copies, waits for them, and re-layouts  3.01 us (4%)
    pallas_call x1, Pallas kernels, per_device(): pl.pallas_call(functools.partial(body, sizes), out_shape=(jax.ShapeDtypeS...  63.2 us
    unnamed x7, local copies, waits for them, and re-layouts  3.01 us

profile of v2, /device:TPU:1, one launch (start us, length us, event | category | flops | bytes accessed | tf_op | source)
XLA Modules:
  0.0 66.9 jit_solution(15773456971884618466)
XLA Ops:
  0.6 63.2 %shard_map.103 = (bf16[32,4,8,32]{3,2,1,0:T(8,128)(2,1)}, f32[16,54]{1,0:T(8,128)}, f32[32,108]{1,0:T(8,128)}) custom-call(bf16[7,8,8,16]{3,2,1,0:T(8,128)(2,1)} %fields_h.1, s32[8,8,16]{2,1,0:T(8,128)} %ids_h.1, bf16[64,128]{1,0:T(8,128)(2,1)} %bitcast.8, bf16[7,64]{1,0:T(8,128)(2,1)} %bitcast.9, bf16[64,1728]{1,0:T(8,128)(2,1)} %k_fine_h.1, ...), custom_call_target="tpu_custom_call" | custom-call | tf_op jit(solution)/shard_map/pallas_call | solution.py:667
  63.9 0.0 copy-start.1
  63.9 1.7 %copy.14 = bf16[32,32,4,8]{1,3,2,0:T(8,128)(2,1)} copy(bf16[32,32,4,8]{1,3,2,0:T(8,128)(2,1)} %bitcast.7) | data formatting | bytes 131072
  65.5 0.0 copy-done.1
  65.5 0.0 copy-start
  65.5 0.6 copy.15
  66.1 0.1 copy-done
  66.3 0.6 copy.16
Async XLA Ops:
  63.9 1.7 %copy-start.1 = (f32[16,54]{1,0:T(8,128)S(1)}, f32[16,54]{1,0:T(8,128)}, u32[]{:S(2)}) copy-start(f32[16,54]{1,0:T(8,128)} %get-tuple-element.13) | copy-start | bytes 10372
  65.5 0.7 %copy-start = (f32[32,108]{1,0:T(8,128)S(1)}, f32[32,108]{1,0:T(8,128)}, u32[]{:S(2)}) copy-start(f32[32,108]{1,0:T(8,128)} %get-tuple-element.14) | copy-start | bytes 41476

commit v3 on v2

--- a/solution.py
+++ b/solution.py
@@ -80,11 +80,12 @@
     ext,
     es,
     af,
+    yf,
     fs,
     fmask,
     kf,
     kd,
-    kb4,
+    kb,
     wblk,
     ac,
     ad,
@@ -94,6 +95,7 @@
     sb,
     slab,
     a3,
+    ysum,
     pre,
     gp,
     gt,
@@ -104,6 +106,7 @@
     zrecv,
     crecv,
     gpad,
+    gpadr,
     ag,
     acts,
     actr,
@@ -156,18 +159,22 @@
         for i, (src, dst) in enumerate(
             [(fields_h, fields), (ids_h, ids), (table_h, table), (w_in_h, w_in), (k_fine_h, k_fine)]
             + [(k_down_h, kd.at[0:1728]), (cot_h, cot)]
-            + [(k_bot_h, kb4.at[32 * q : 32 * q + 32]) for q in range(4)]
+            + [
+                (k_bot_h.at[:, x * 1152 : x * 1152 + 1152], kb.at[32 * x : 32 * x + 32])
+                for x in range(3)
+            ]
         )
     ]
     for c in loads:
         c.start()
     kd[1728:1792, :] = jnp.zeros((64, 128), BF16)
+    kb[96:128, :] = jnp.zeros((32, 1152), BF16)
     kf[...] = jnp.zeros(kf.shape, BF16)
     wblk[...] = jnp.zeros(wblk.shape, BF16)
     fs[...] = jnp.zeros(fs.shape, F32)
     gpad[...] = jnp.zeros(gpad.shape, F32)
     slab[0] = jnp.zeros((64, 128), F32)
-    slab[4 * nx + 1] = jnp.zeros((64, 128), F32)
+    slab[4 * nx + 1 : 4 * nx + 4] = jnp.zeros((3, 64, 128), F32)
     cb[...] = jnp.zeros(cb.shape, F32)
     cotf[...] = jnp.zeros(cotf.shape, F32)
     ext[:, :, 6:8] = jnp.zeros((11, 4, 2, 1, 128), F32)
@@ -195,12 +202,18 @@
 
     for c in loads[2:]:
         c.wait()
-    kf[0:64, 0:1728] = k_fine[...]
-    kf[64:128, 0:1728] = k_fine[...]
+    lane = lane_iota((64, 640))
+    first = jnp.where(lane < 576, k_fine[:, 0:640].astype(F32), 0.0)
+    second = pltpu.roll(k_fine[:, 512:1152].astype(F32), 576, 1)
+    kf[0:64, :] = first.astype(BF16)
+    kf[64:128, :] = jnp.where(lane < 576, second, 0.0).astype(BF16)
+    for n in (128, 192):
+        kf[n : n + 64, 0:576] = k_fine[:, 1152:1728]
     for t in range(27):
-        for q in range(4):
-            wblk[t * 128 + q * 32 : t * 128 + q * 32 + 32, q * 128 : q * 128 + 128] = kb4[
-                0:32, t * 128 : t * 128 + 128
+        for q in range(2):
+            row = t * 64 + q * 32
+            wblk[row : row + 32, q * 128 : q * 128 + 128] = kb[
+                (t // 9) * 32 : (t // 9) * 32 + 32, (t % 9) * 128 : (t % 9) * 128 + 128
             ]
     my = gy * 8 - 3 + lax.broadcasted_iota(jnp.int32, (13, 24, 128), 0)
     mz = gz * 16 - 3 + lax.broadcasted_iota(jnp.int32, (13, 24, 128), 1)
@@ -232,7 +245,7 @@
 
     row8 = lax.broadcasted_iota(jnp.int32, (128, 7), 0) % 8
     pick = jnp.where(row8 == lax.broadcasted_iota(jnp.int32, (128, 7), 1), 1.0, 0.0).astype(BF16)
-    emb_row = lax.broadcasted_iota(jnp.int32, (128, 256), 0) // 8
+    emb_lane = lane_iota((128, 128)) // 8
     twice = jnp.where(
         lax.broadcasted_iota(jnp.int32, (64, 128), 1) % 64
         == lax.broadcasted_iota(jnp.int32, (64, 128), 0),
@@ -241,8 +254,7 @@
     ).astype(BF16)
     w_rows = dot(pick, dot(w_in[...], twice).astype(BF16))
     table2 = jnp.concatenate([table[...]] * 2, axis=0)
-    id_rows = jnp.where(lax.broadcasted_iota(jnp.int32, (128, 128), 0) % 8 == 7, 1.0, 0.0)
-    w_emb = jnp.concatenate([id_rows, w_rows], axis=1)
+    w_cols = jnp.transpose(w_rows)
 
     own.wait()
     for c in halo:
@@ -257,28 +269,40 @@
     outside = outside | ((by == 0) & (gy == 0)) | ((by == 3) & (gy == ny - 1))
     outside = outside | ((bz == 0) & (gz == 0)) | ((bz == 5) & (gz == nz - 1))
     fill = jnp.where(lane_iota((44, 8, 128)) % 8 == 7, -1.0, 0.0)
-    blocks = jnp.where(outside, fill, blocks).reshape(352, 128).astype(BF16)
+    blocks = jnp.where(outside, fill, blocks).reshape(352, 128)
+    components = blocks.astype(BF16)
     lanes = lane_iota((352, 128)).astype(F32)
     for p in range(16):
         y4, z4 = p // 4, p % 4
-        w_p = jnp.where(emb_row == p, w_emb, 0.0).astype(BF16)
-        both = dot(blocks, w_p)
-        onehot = jnp.where(both[:, 0:128] == lanes, 1.0, 0.0).astype(BF16)
-        value = silu(both[:, 128:256] + dot_nt(onehot, table2)).reshape(11, 4, 8, 128)
+        w_p = jnp.where(emb_lane == p, w_cols, 0.0).astype(BF16)
+        grain = jnp.broadcast_to(blocks[:, p * 8 + 7 : p * 8 + 8], (352, 128))
+        onehot = jnp.where(grain == lanes, 1.0, 0.0).astype(BF16)
+        both = jnp.concatenate([onehot, components], axis=1)
+        value = silu(dot_nt(both, jnp.concatenate([table2, w_p], axis=1)))
+        value = value.reshape(11, 4, 8, 128)
         for x in range(11):
             for yb in range(4):
                 es[x, yb * 4 + y4, pl.ds(z4, 8, stride=4), :] = value[x, yb]
 
     half = lane_iota((13, 24, 128)) < 64
 
-    def fine_plane(x, carry):
-        for t in range(14):
-            (ax, ay, az), (bx_, by_, bz_) = tap_of(2 * t), tap_of(2 * t + 1)
-            low = es[x + ax, ay : ay + 13, az : az + 24, :]
-            high = es[x + bx_, by_ : by_ + 13, bz_ : bz_ + 24, :]
+    def spread_plane(e):
+        for t in range(5):
+            ay, az = (2 * t) // 3, (2 * t) % 3
+            by_, bz_ = min(2 * t + 1, 8) // 3, min(2 * t + 1, 8) % 3
+            low = es[e, ay : ay + 13, az : az + 24, :]
+            high = es[e, by_ : by_ + 13, bz_ : bz_ + 24, :]
             block = jnp.where(half, low, high)
             af[:, t * 128 : t * 128 + 128] = block.reshape(312, 128).astype(BF16)
-        value = silu(dot_nt(af[...], kf[...])).reshape(13, 24, 128)
+        yf[e] = dot_nt(af[...], kf[...])
+
+    half_rows = lane_iota((312, 128)) < 64
+
+    def fine_plane(x, carry):
+        spread_plane(x + 2)
+        two = jnp.where(half_rows, yf[x, :, 0:128], yf[x + 1, :, 0:128])
+        value = two + pltpu.roll(two, 64, 1) + yf[x + 2, :, 128:256]
+        value = silu(value).reshape(13, 24, 128)
         keep = jnp.where((x > 0) | (gx > 0), 1.0, 0.0)
         value = value * fmask[...] * keep
         fs[x, :, 0:24, :] = value.astype(BF16).astype(F32)
@@ -318,19 +342,24 @@
             coarse_copy(x, k).start()
         return carry
 
+    def first_planes(e, carry):
+        spread_plane(e)
+        return carry
+
+    lax.fori_loop(0, 2, first_planes, 0)
     fine_plane(0, 0)
     lax.fori_loop(0, 4, coarse_plane, 0)
 
     half8 = lane_iota((8, 128)) < 64
-    for y in range(4):
+    for x in range(4):
         for t in range(14):
             (ax, ay, az), (bx_, by_, bz_) = tap_of(2 * t), tap_of(2 * t + 1)
             parts = []
-            for x in range(4):
+            for y in range(4):
                 low = fs[2 * x + ax, 2 * y + 2 + ay, pl.ds(2 + az, 8, stride=2), :]
                 high = fs[2 * x + bx_, 2 * y + 2 + by_, pl.ds(2 + bz_, 8, stride=2), :]
                 parts.append(jnp.where(half8, low, high))
-            ad[y * 32 : y * 32 + 32, t * 128 : t * 128 + 128] = jnp.concatenate(parts, axis=0).astype(BF16)
+            ad[x * 32 : x * 32 + 32, t * 128 : t * 128 + 128] = jnp.concatenate(parts, axis=0).astype(BF16)
 
     slab[pl.ds(1 + gx * 4, 4)] = cs[...].astype(F32)
 
@@ -342,7 +371,7 @@
         for z in range(8):
             rows = cotf[pl.ds(y * 8 + z, 32, stride=32), :]
             rows = jnp.concatenate([jnp.where(group == q, rows, 0.0) for q in range(4)], axis=0)
-            cotp[y, pl.ds(z, 8, stride=8), :] = dot_nt(spread, rows.astype(BF16))
+            cotp[pl.ds(y * 8 + z, 8, stride=32), :] = dot_nt(spread, rows.astype(BF16))
 
     for k in range(1, nx):
         for x in range(4):
@@ -350,33 +379,40 @@
         source = lax.rem(gx - k + nx, nx)
         slab[pl.ds(1 + source * 4, 4)] = sb[source].astype(F32)
 
-    for y in range(4):
-        for t in range(27):
-            ax, ay, az = tap_of(t)
-            start = (y + ay) * 10 + az
-            window = slab[ax : ax + 32, start : start + 8, :].reshape(4, 64, 128).astype(BF16)
-            a3[:, y * 64 : y * 64 + 64, t * 128 : t * 128 + 128] = window
-
-    def bottle_group(q, carry):
-        pre[q] = dot_nt(a3[q], kb4[...])
+    for pair in range(2):
+        for t in range(9):
+            start = (2 * pair + t // 3) * 10 + t % 3
+            window = [slab[:, start : start + 8, :], slab[:, start + 10 : start + 18, :]]
+            window = jnp.concatenate(window, axis=1).astype(BF16)
+            a3[:, pair * 16 : pair * 16 + 16, t * 128 : t * 128 + 128] = window
+
+    def bottle_planes(c, carry):
+        part = a3[pl.ds(c * 9, 9)].reshape(288, 1152)
+        ysum[pl.ds(c * 9, 9)] = dot_nt(part, kb[...]).reshape(9, 32, 128)
         return carry
 
-    lax.fori_loop(0, 4, bottle_group, 0)
+    lax.fori_loop(0, 4, bottle_planes, 0)
     group = lane_iota((256, 128)) // 32
-    z = pre[0]
-    for q in range(1, 4):
-        z = jnp.where(group == q, pre[q], z)
-    grad = cotp[...].reshape(256, 128) * silu_grad(z)
+    z = None
+    for ax in range(3):
+        term = None
+        for q in range(4):
+            rows = ysum[8 * q + ax : 8 * q + ax + 8].reshape(256, 128)
+            shift = ((q - ax) * 32) % 128
+            rows = rows if shift == 0 else pltpu.roll(rows, shift, 1)
+            term = rows if term is None else jnp.where(group == q, rows, term)
+        z = term if z is None else z + term
+    pre[...] = z
+    grad = cotp[...] * silu_grad(z)
     grad = grad.astype(BF16).astype(F32)
-    gp[...] = grad.reshape(4, 64, 128)
+    gp[...] = grad
 
     for side in range(2):
-        ysend[side] = gp[3 - 3 * side].astype(BF16)
-        zsend[side] = jnp.concatenate(
-            [gp[y, pl.ds(7 - 7 * side, 8, stride=8), :] for y in range(4)], axis=0
-        ).astype(BF16)
+        row = 3 - 3 * side
+        ysend[side] = grad.reshape(8, 32, 128)[:, row * 8 : row * 8 + 8].reshape(64, 128).astype(BF16)
+        zsend[side] = gp[pl.ds(7 - 7 * side, 32, stride=8), :].astype(BF16)
         for other in range(2):
-            corner = gp[3 - 3 * side, pl.ds(7 - 7 * other, 8, stride=8), :]
+            corner = gp[pl.ds(row * 8 + 7 - 7 * other, 8, stride=32), :]
             csend[side * 2 + other] = jnp.concatenate([corner, corner], axis=0).astype(BF16)
     rim = []
 
@@ -405,15 +441,21 @@
             1 - 2 * (corner % 2),
         )
 
-    gt[...] = jnp.transpose(grad).astype(BF16)
-    for n in range(9):
-        total = None
-        for q in range(4):
-            part = dot(gt[32 * q : 32 * q + 32, :], a3[q, :, n * 384 : n * 384 + 384])
-            total = part if total is None else total + part
-        gball[:, n * 384 : n * 384 + 384] = total * scale
+    turned = jnp.transpose(grad)
+    turned = [turned[32 * q : 32 * q + 32] for q in range(4)] + [jnp.zeros((32, 128), F32)]
+    turned = jnp.concatenate(turned, axis=1)
+    turned = [turned, pltpu.roll(turned, 32, 1), pltpu.roll(turned, 64, 1)]
+    gt[...] = jnp.concatenate(turned, axis=0).astype(BF16)
+    for n in range(3):
+        columns_n = a3[:, :, n * 384 : n * 384 + 384].reshape(1152, 384)
+        gball[:, n * 384 : n * 384 + 384] = dot(gt[...], columns_n) * scale
+
+    def gball_tile(tile):
+        row, lane = (tile // 9) * 32, (tile % 9) * 128
+        return gball[row : row + 32, lane : lane + 128]
+
     for k in range(ny * nz):
-        cut = piece(lambda tile: gball[:, tile * 128 : tile * 128 + 128], 108 * k, 108)
+        cut = piece(gball_tile, 108 * k, 108)
         gbs[k % nz, k // nz] = cut.astype(BF16)
     me = gy * nz + gz
     gb_copies = []
@@ -430,7 +472,7 @@
             )
         )
 
-    gpad[1:5, 1:9, 1:9, :] = gp[...].reshape(4, 8, 8, 128)
+    gpad[1:9, 1:5, 1:9, :] = gp[...].reshape(8, 4, 8, 128)
     for c in rim:
         c.wait()
     for c in gb_copies:
@@ -442,23 +484,29 @@
     y_ok = (gy > 0, gy < ny - 1)
     z_ok = (gz > 0, gz < nz - 1)
     for side in range(2):
-        gpad[5 * side, 1:9, 1:9, :] = kept(y_ok[side], yrecv[side]).reshape(8, 8, 128)
+        gpad[1:9, 5 * side, 1:9, :] = kept(y_ok[side], yrecv[side]).reshape(8, 8, 128)
         value = kept(z_ok[side], zrecv[side])
-        for y in range(4):
-            gpad[1 + y, 1:9, 9 * side : 9 * side + 1, :] = value[8 * y : 8 * y + 8].reshape(8, 1, 128)
+        gpad[1:9, 1:5, 9 * side : 9 * side + 1, :] = value.reshape(8, 4, 1, 128)
         for other in range(2):
             value = kept(y_ok[side] & z_ok[other], crecv[side * 2 + other])
-            gpad[5 * side, 1:9, 9 * other : 9 * other + 1, :] = value[0:8].reshape(8, 1, 128)
+            gpad[1:9, 5 * side, 9 * other : 9 * other + 1, :] = value[0:8].reshape(8, 1, 128)
     edge = lane_iota((96, 128))
-    low = pltpu.roll(gpad[:, 8, :, :].reshape(96, 128), 32, 1)
-    gpad[:, 0, :, :] = jnp.where(edge < 32, 0.0, low).reshape(6, 16, 128)
-    high = pltpu.roll(gpad[:, 1, :, :].reshape(96, 128), 96, 1)
-    gpad[:, 9, :, :] = jnp.where(edge >= 96, 0.0, high).reshape(6, 16, 128)
-
-    for t in range(27):
+    low = pltpu.roll(gpad[8].reshape(96, 128), 32, 1)
+    gpad[0] = jnp.where(edge < 32, 0.0, low).reshape(6, 16, 128)
+    high = pltpu.roll(gpad[1].reshape(96, 128), 96, 1)
+    gpad[9] = jnp.where(edge >= 96, 0.0, high).reshape(6, 16, 128)
+    gpadr[...] = pltpu.roll(gpad[...].reshape(960, 128), 64, 1).reshape(10, 6, 16, 128)
+
+    def grad_window(ref, t):
         ax, ay, az = tap_of(t)
-        window = gpad[2 - ay : 6 - ay, 2 - ax : 10 - ax, 2 - az : 10 - az, :]
-        ag[:, t * 128 : t * 128 + 128] = window.reshape(256, 128).astype(BF16)
+        window = ref[2 - ax : 10 - ax, 2 - ay : 6 - ay, 2 - az : 10 - az, :]
+        return window.reshape(256, 128)
+
+    half_rows = lane_iota((256, 128)) < 64
+    for t in range(14):
+        for pair, (one, two) in enumerate([(gpad, gpadr), (gpadr, gpad)]):
+            window = jnp.where(half_rows, grad_window(one, 2 * t), grad_window(two, 2 * t + 1))
+            ag[pair, :, t * 128 : t * 128 + 128] = window.astype(BF16)
     def act_copy(slot, target, source):
         return pltpu.make_async_remote_copy(
             src_ref=acts.at[target],
@@ -469,23 +517,20 @@
             device_id_type=MESH,
         )
 
-    for q in range(4):
-        act = dot(ag[...], wblk[:, q * 128 : q * 128 + 128]).reshape(4, 64, 128).astype(BF16)
-        for part in range(2):
-            target = 2 * q + part
-            acts[target] = act[:, part * 32 : part * 32 + 32, :]
+    for pair in range(2):
+        act = dot(ag[pair], wblk[...]).astype(BF16)
+        for part in range(4):
+            target = 4 * pair + part
+            row, lane = (part % 2) * 128, (part // 2) * 128
+            acts[target] = act[row : row + 128, lane : lane + 128]
 
             @pl.when(gx != target)
             def _(target=target):
                 act_copy(gx, target, gx).start()
 
-    z = pre[0]
-    group = lane_iota((256, 128)) // 32
-    for q in range(1, 4):
-        z = jnp.where(group == q, pre[q], z)
-    out = silu(z).astype(BF16).astype(F32).reshape(4, 64, 128)
+    out = silu(pre[...]).astype(BF16).astype(F32).reshape(8, 4, 8, 128)
     for y in range(4):
-        turned = jnp.transpose(jnp.concatenate([out[y], jnp.zeros((64, 128), F32)], axis=0))
+        turned = jnp.transpose(jnp.concatenate([out[:, y].reshape(64, 128), jnp.zeros((64, 128), F32)], axis=0))
         for q in range(4):
             tt[y * 32 : y * 32 + 32, q * 128 : q * 128 + 128] = turned[q * 32 : q * 32 + 32].astype(BF16)
     row = lax.broadcasted_iota(jnp.int32, (512, 128), 0)
@@ -498,17 +543,14 @@
             bo[pl.ds(y * 8 + k, 32, stride=32), :] = turned[y * 32 : y * 32 + 32]
     bottle_o[...] = bo[...].reshape(32, 4, 8, 128)[:, :, :, 0:32].astype(BF16)
 
-    slope = []
-    for y in range(4):
-        for x in range(4):
-            slope.append(silu_grad(pd[x, y + 1, 1:9, :]))
+    slope = [silu_grad(pd[x, y + 1, 1:9, :]) for x in range(4) for y in range(4)]
     slope = jnp.concatenate(slope, axis=0)
     total = acts[gx].astype(F32)
     for k in range(1, nx):
         source = lax.rem(gx - k + nx, nx)
         act_copy(source, lax.rem(gx + k, nx), source).wait()
         total = total + actr[source].astype(F32)
-    grad_down = (total.reshape(128, 128) * slope).astype(BF16).astype(F32)
+    grad_down = (total * slope).astype(BF16).astype(F32)
     grad_down_t = jnp.transpose(grad_down).astype(BF16)
 
     part = dot(grad_down_t, ad[...]) * scale
@@ -601,45 +643,48 @@
         V((64, 1728), BF16),
         V((32, 4, 8, 32), BF16),
         V((1024, 128), F32),
-        V((4, 64, 128), F32),
+        V((256, 128), F32),
         V((128, 512), BF16),
         V((1024, 128), F32),
         V((64, 128), F32),
         V((8, 2, 4, 1, 128), F32),
         V((11, 4, 8, 1, 128), F32),
         V((11, 16, 32, 128), F32),
-        V((312, 1792), BF16),
+        V((312, 640), BF16),
+        V((11, 312, 256), F32),
         V((9, 13, 40, 128), F32),
         V((13, 24, 128), F32),
-        V((128, 1792), BF16),
+        V((256, 640), BF16),
         V((1792, 128), BF16),
-        V((128, 3456), BF16),
-        V((3456, 512), BF16),
+        V((128, 1152), BF16),
+        V((1792, 256), BF16),
         V((96, 1792), BF16),
         V((128, 1792), BF16),
         V((4, 6, 16, 128), F32),
         V((4, 64, 128), F32),
         V((4, 64, 128), BF16),
         V((nx, 4, 64, 128), BF16),
-        V((4 * nx + 2, 64, 128), F32),
-        V((4, 256, 3456), BF16),
-        V((4, 256, 128), F32),
-        V((4, 64, 128), F32),
-        V((128, 256), BF16),
+        V((4 * nx + 4, 64, 128), F32),
+        V((36, 32, 1152), BF16),
+        V((36, 32, 128), F32),
+        V((256, 128), F32),
+        V((256, 128), F32),
+        V((96, 1152), BF16),
         V((2, 64, 128), BF16),
         V((2, 32, 128), BF16),
         V((4, 16, 128), BF16),
         V((2, 64, 128), BF16),
         V((2, 32, 128), BF16),
         V((4, 16, 128), BF16),
-        V((6, 10, 16, 128), F32),
-        V((256, 3456), BF16),
-        V((nx, 4, 32, 128), BF16),
-        V((nx, 4, 32, 128), BF16),
+        V((10, 6, 16, 128), F32),
+        V((10, 6, 16, 128), F32),
+        V((2, 256, 1792), BF16),
+        V((nx, 128, 128), BF16),
+        V((nx, 128, 128), BF16),
         V((nx, 16, 1792), BF16),
         V((nx, 16, 1792), BF16),
         V((16, 1792), F32),
-        V((32, 3456), F32),
+        V((96, 1152), F32),
         V((nz, ny, 32, 128), BF16),
         V((nz, ny, 32, 128), BF16),
         V((ny, 32, 128), BF16),

time: 67.1 us -> 63.2 us (0.942)
  Pallas kernels: 63.2 us -> 59.4 us
    pallas_call x1, Pallas kernels: 63.2 us -> 59.4 us  [per_device(): pl.pallas_call(functools.partial(body, sizes), out_shape=(jax.ShapeDtypeS...]
where the time goes in v3:
time: 63.2 us; the launch traced here: 63 us
  Pallas kernels  59.4 us (94%)
  local copies, waits for them, and re-layouts  3.01 us (5%)
  between operations  0.65 us (1%)
    pallas_call x1, Pallas kernels, per_device(): pl.pallas_call(functools.partial(body, sizes), out_shape=(jax.ShapeDtypeS...  59.4 us
    unnamed x7, local copies, waits for them, and re-layouts  3.01 us

profile of v3, /device:TPU:1, one launch (start us, length us, event | category | flops | bytes accessed | tf_op | source)
XLA Modules:
  0.0 63.0 jit_solution(14677470913966096336)
XLA Ops:
  0.6 59.4 %shard_map.103 = (bf16[32,4,8,32]{3,2,1,0:T(8,128)(2,1)}, f32[16,54]{1,0:T(8,128)}, f32[32,108]{1,0:T(8,128)}) custom-call(bf16[7,8,8,16]{3,2,1,0:T(8,128)(2,1)} %fields_h.1, s32[8,8,16]{2,1,0:T(8,128)} %ids_h.1, bf16[64,128]{1,0:T(8,128)(2,1)} %bitcast.8, bf16[7,64]{1,0:T(8,128)(2,1)} %bitcast.9, bf16[64,1728]{1,0:T(8,128)(2,1)} %k_fine_h.1, ...), custom_call_target="tpu_custom_call" | custom-call | tf_op jit(solution)/shard_map/pallas_call | solution.py:712
  60.0 0.0 copy-start.1
  60.0 1.7 %copy.14 = bf16[32,32,4,8]{1,3,2,0:T(8,128)(2,1)} copy(bf16[32,32,4,8]{1,3,2,0:T(8,128)(2,1)} %bitcast.7) | data formatting | bytes 131072
  61.7 0.0 copy-done.1
  61.7 0.0 copy-start
  61.7 0.6 copy.15
  62.3 0.1 copy-done
  62.4 0.6 copy.16
Async XLA Ops:
  60.0 1.7 %copy-start.1 = (f32[16,54]{1,0:T(8,128)S(1)}, f32[16,54]{1,0:T(8,128)}, u32[]{:S(2)}) copy-start(f32[16,54]{1,0:T(8,128)} %get-tuple-element.13) | copy-start | bytes 10372
  61.7 0.7 %copy-start = (f32[32,108]{1,0:T(8,128)S(1)}, f32[32,108]{1,0:T(8,128)}, u32[]{:S(2)}) copy-start(f32[32,108]{1,0:T(8,128)} %get-tuple-element.14) | copy-start | bytes 41476

commit v4 on v3

--- a/solution.py
+++ b/solution.py
@@ -150,6 +150,7 @@
     columns = [(dx, 0, 0) for dx in range(1, nx)]
     planes = [(0, dy, dz) for dy in range(ny) for dz in range(nz) if (dy, dz) != (0, 0)]
     partners = sorted({(a % nx, b % ny, c % nz) for a, b, c in near + columns + planes})
+    partners.sort(key=lambda p: -2 * min(p[1], ny - p[1]) - min(p[2], nz - p[2]) - min(p[0], nx - p[0]))
     barrier = pltpu.get_barrier_semaphore()
     for p in partners:
         pl.semaphore_signal(barrier, inc=1, device_id=device(*p), device_id_type=MESH)
@@ -173,8 +174,10 @@
     wblk[...] = jnp.zeros(wblk.shape, BF16)
     fs[...] = jnp.zeros(fs.shape, F32)
     gpad[...] = jnp.zeros(gpad.shape, F32)
-    slab[0] = jnp.zeros((64, 128), F32)
-    slab[4 * nx + 1 : 4 * nx + 4] = jnp.zeros((3, 64, 128), F32)
+    a3[0] = jnp.zeros((32, 1152), BF16)
+    a3[4 * nx + 1 : 4 * nx + 4] = jnp.zeros((3, 32, 1152), BF16)
+    ysum[0] = jnp.zeros((32, 128), F32)
+    ysum[4 * nx + 1] = jnp.zeros((32, 128), F32)
     cb[...] = jnp.zeros(cb.shape, F32)
     cotf[...] = jnp.zeros(cotf.shape, F32)
     ext[:, :, 6:8] = jnp.zeros((11, 4, 2, 1, 128), F32)
@@ -257,32 +260,40 @@
     w_cols = jnp.transpose(w_rows)
 
     own.wait()
-    for c in halo:
-        c.wait()
-
-    blocks = ext[...].reshape(44, 8, 128)
-    bx = lax.broadcasted_iota(jnp.int32, (44, 8, 128), 0)
-    by = bx % 4
-    bx = bx // 4
-    bz = lax.broadcasted_iota(jnp.int32, (44, 8, 128), 1)
-    outside = ((bx < 2) & (gx == 0)) | ((bx == 10) & (gx == nx - 1))
-    outside = outside | ((by == 0) & (gy == 0)) | ((by == 3) & (gy == ny - 1))
+    for c, n in zip(halo, near):
+        if n[0] == 0:
+            c.wait()
+
+    by = lax.broadcasted_iota(jnp.int32, (4, 8, 128), 0)
+    bz = lax.broadcasted_iota(jnp.int32, (4, 8, 128), 1)
+    outside = ((by == 0) & (gy == 0)) | ((by == 3) & (gy == ny - 1))
     outside = outside | ((bz == 0) & (gz == 0)) | ((bz == 5) & (gz == nz - 1))
-    fill = jnp.where(lane_iota((44, 8, 128)) % 8 == 7, -1.0, 0.0)
-    blocks = jnp.where(outside, fill, blocks).reshape(352, 128)
-    components = blocks.astype(BF16)
-    lanes = lane_iota((352, 128)).astype(F32)
-    for p in range(16):
-        y4, z4 = p // 4, p % 4
-        w_p = jnp.where(emb_lane == p, w_cols, 0.0).astype(BF16)
-        grain = jnp.broadcast_to(blocks[:, p * 8 + 7 : p * 8 + 8], (352, 128))
-        onehot = jnp.where(grain == lanes, 1.0, 0.0).astype(BF16)
-        both = jnp.concatenate([onehot, components], axis=1)
-        value = silu(dot_nt(both, jnp.concatenate([table2, w_p], axis=1)))
-        value = value.reshape(11, 4, 8, 128)
-        for x in range(11):
-            for yb in range(4):
-                es[x, yb * 4 + y4, pl.ds(z4, 8, stride=4), :] = value[x, yb]
+    fill = jnp.where(lane_iota((4, 8, 128)) % 8 == 7, -1.0, 0.0)
+
+    def embed(planes_x):
+        rows = len(planes_x) * 32
+        blocks = []
+        for x in planes_x:
+            block = jnp.where(outside, fill, ext[x].reshape(4, 8, 128))
+            if x < 2:
+                block = jnp.where(gx == 0, fill, block)
+            if x == 10:
+                block = jnp.where(gx == nx - 1, fill, block)
+            blocks.append(block)
+        blocks = jnp.concatenate(blocks, axis=0).reshape(rows, 128)
+        components = blocks.astype(BF16)
+        lanes = lane_iota((rows, 128)).astype(F32)
+        for p in range(16):
+            y4, z4 = p // 4, p % 4
+            w_p = jnp.where(emb_lane == p, w_cols, 0.0).astype(BF16)
+            grain = jnp.broadcast_to(blocks[:, p * 8 + 7 : p * 8 + 8], (rows, 128))
+            onehot = jnp.where(grain == lanes, 1.0, 0.0).astype(BF16)
+            both = jnp.concatenate([onehot, components], axis=1)
+            value = silu(dot_nt(both, jnp.concatenate([table2, w_p], axis=1)))
+            value = value.reshape(len(planes_x), 4, 8, 128)
+            for i, x in enumerate(planes_x):
+                for yb in range(4):
+                    es[x, yb * 4 + y4, pl.ds(z4, 8, stride=4), :] = value[i, yb]
 
     half = lane_iota((13, 24, 128)) < 64
 
@@ -298,15 +309,18 @@
 
     half_rows = lane_iota((312, 128)) < 64
 
-    def fine_plane(x, carry):
+    def next_plane(x, carry):
         spread_plane(x + 2)
+        fine_plane(x)
+        return carry
+
+    def fine_plane(x):
         two = jnp.where(half_rows, yf[x, :, 0:128], yf[x + 1, :, 0:128])
         value = two + pltpu.roll(two, 64, 1) + yf[x + 2, :, 128:256]
         value = silu(value).reshape(13, 24, 128)
         keep = jnp.where((x > 0) | (gx > 0), 1.0, 0.0)
         value = value * fmask[...] * keep
         fs[x, :, 0:24, :] = value.astype(BF16).astype(F32)
-        return carry
 
     def coarse_copy(x, k):
         return pltpu.make_async_remote_copy(
@@ -324,7 +338,7 @@
     inside = (cy >= 0) & (cy < ny * 4) & (cz >= 0) & (cz < nz * 8)
 
     def coarse_plane(x, carry):
-        lax.fori_loop(2 * x + 1, 2 * x + 3, fine_plane, 0)
+        lax.fori_loop(2 * x + 1, 2 * x + 3, next_plane, 0)
         for y in range(6):
             row = y * 16
             for t in range(14):
@@ -338,16 +352,24 @@
         for y in range(6):
             cb[x, y * 10 : y * 10 + 10, :] = coarse[y, 0:10, :]
         cs[x] = cb[x].astype(BF16)
+        sb[gx, x] = cb[x].astype(BF16)
         for k in range(1, nx):
             coarse_copy(x, k).start()
         return carry
 
+    embed(range(2, 10))
+    spread_plane(2)
+    for c, n in zip(halo, near):
+        if n[0] != 0:
+            c.wait()
+    embed((0, 1, 10))
+
     def first_planes(e, carry):
         spread_plane(e)
         return carry
 
     lax.fori_loop(0, 2, first_planes, 0)
-    fine_plane(0, 0)
+    fine_plane(0)
     lax.fori_loop(0, 4, coarse_plane, 0)
 
     half8 = lane_iota((8, 128)) < 64
@@ -361,7 +383,6 @@
                 parts.append(jnp.where(half8, low, high))
             ad[x * 32 : x * 32 + 32, t * 128 : t * 128 + 128] = jnp.concatenate(parts, axis=0).astype(BF16)
 
-    slab[pl.ds(1 + gx * 4, 4)] = cs[...].astype(F32)
 
     cotf[:, 0:32] = cot[...].astype(F32).reshape(1024, 32)
     group = lane_iota((32, 128)) // 8
@@ -373,25 +394,24 @@
             rows = jnp.concatenate([jnp.where(group == q, rows, 0.0) for q in range(4)], axis=0)
             cotp[pl.ds(y * 8 + z, 8, stride=32), :] = dot_nt(spread, rows.astype(BF16))
 
-    for k in range(1, nx):
-        for x in range(4):
+    def bottle_plane(x, carry):
+        for k in range(1, nx):
             coarse_copy(x, k).wait()
-        source = lax.rem(gx - k + nx, nx)
-        slab[pl.ds(1 + source * 4, 4)] = sb[source].astype(F32)
-
-    for pair in range(2):
-        for t in range(9):
-            start = (2 * pair + t // 3) * 10 + t % 3
-            window = [slab[:, start : start + 8, :], slab[:, start + 10 : start + 18, :]]
-            window = jnp.concatenate(window, axis=1).astype(BF16)
-            a3[:, pair * 16 : pair * 16 + 16, t * 128 : t * 128 + 128] = window
-
-    def bottle_planes(c, carry):
-        part = a3[pl.ds(c * 9, 9)].reshape(288, 1152)
-        ysum[pl.ds(c * 9, 9)] = dot_nt(part, kb[...]).reshape(9, 32, 128)
+        slab[...] = sb[:, x].astype(F32)
+        for pair in range(2):
+            for t in range(9):
+                start = (2 * pair + t // 3) * 10 + t % 3
+                window = [slab[:, start : start + 8, :], slab[:, start + 10 : start + 18, :]]
+                window = jnp.concatenate(window, axis=1).astype(BF16)
+                for n in range(nx):
+                    a3[1 + 4 * n + x, pair * 16 : pair * 16 + 16, t * 128 : t * 128 + 128] = window[n]
+        part = jnp.concatenate([a3[1 + 4 * n + x] for n in range(nx)], axis=0)
+        part = dot_nt(part, kb[...]).reshape(nx, 32, 128)
+        for n in range(nx):
+            ysum[1 + 4 * n + x] = part[n]
         return carry
 
-    lax.fori_loop(0, 4, bottle_planes, 0)
+    lax.fori_loop(0, 4, bottle_plane, 0)
     group = lane_iota((256, 128)) // 32
     z = None
     for ax in range(3):
@@ -626,6 +646,17 @@
         total = total + gdr[source].astype(F32)
     gdown_o[0:8, :] = total[:, 0:54]
     gdown_o[8:16, :] = pltpu.roll(total, 64, 1)[:, 0:54]
+
+
+def put_out(a, b, c, a_out, b_out, c_out, sems):
+    copies = [
+        pltpu.make_async_copy(source, out, sems.at[i])
+        for i, (source, out) in enumerate([(a, a_out), (b, b_out), (c, c_out)])
+    ]
+    for copy in copies:
+        copy.start()
+    for copy in copies:
+        copy.wait()
 
 
 def per_device(sizes, fields, grain_ids, table, w_in, k_fine, k_down, k_bot, cotangent):
@@ -664,7 +695,7 @@
         V((4, 64, 128), F32),
         V((4, 64, 128), BF16),
         V((nx, 4, 64, 128), BF16),
-        V((4 * nx + 4, 64, 128), F32),
+        V((nx, 64, 128), F32),
         V((36, 32, 1152), BF16),
         V((36, 32, 128), F32),
         V((256, 128), F32),
@@ -712,9 +743,9 @@
     bottle, grad_down, grad_bottle = pl.pallas_call(
         functools.partial(body, sizes),
         out_shape=(
-            jax.ShapeDtypeStruct((32, 4, 8, 32), BF16),
-            jax.ShapeDtypeStruct((16, 54), F32),
-            jax.ShapeDtypeStruct((32, 108), F32),
+            V((32, 4, 8, 32), BF16),
+            V((16, 54), F32),
+            V((32, 108), F32),
         ),
         in_specs=[pl.BlockSpec(memory_space=pl.ANY)] * 8,
         out_specs=(vmem, vmem, vmem),
@@ -723,6 +754,18 @@
             collective_id=0, has_side_effects=True, vmem_limit_bytes=60 * 1024 * 1024
         ),
     )(fields, grain_ids, table.T, w_in.T, k_fine, k_down.T, k_bot, cot)
+    bottle, grad_down, grad_bottle = pl.pallas_call(
+        put_out,
+        out_shape=(
+            jax.ShapeDtypeStruct((32, 4, 8, 32), BF16),
+            jax.ShapeDtypeStruct((16, 54), F32),
+            jax.ShapeDtypeStruct((32, 108), F32),
+        ),
+        in_specs=[vmem] * 3,
+        out_specs=[pl.BlockSpec(memory_space=pl.ANY)] * 3,
+        scratch_shapes=[D((3,))],
+        compiler_params=pltpu.CompilerParams(vmem_limit_bytes=1024 * 1024),
+    )(bottle, grad_down, grad_bottle)
     return bottle.transpose(0, 3, 1, 2), grad_down, grad_bottle
 
 

time: 63.2 us -> 58.2 us (0.921)
  local copies, waits for them, and re-layouts: 3.01 us -> 0 us
  Pallas kernels: 59.4 us -> 57.5 us
    unnamed x7 -> x0, local copies, waits for them, and re-layouts: 3.01 us -> none
    pallas_call x1 -> x2, Pallas kernels: 59.4 us -> 57.5 us  [the longest x1 56.8 us: per_device(): pl.pallas_call(functools.partial(body, sizes), out_shape=(V((32, 4, 8, 32...]
where the time goes in v4:
time: 58.2 us; the launch traced here: 58.1 us
  Pallas kernels  57.5 us (99%)
  between operations  0.64 us (1%)
    pallas_call x1, Pallas kernels, per_device(): pl.pallas_call(functools.partial(body, sizes), out_shape=(V((32, 4, 8, 32...  56.8 us

profile of v4, /device:TPU:1, one launch (start us, length us, event | category | flops | bytes accessed | tf_op | source)
XLA Modules:
  0.0 58.1 jit_solution(16633357622941052501)
XLA Ops:
  0.6 56.8 %shard_map.103 = (bf16[32,4,8,32]{3,2,1,0:T(8,128)(2,1)S(1)}, f32[16,54]{1,0:T(8,128)S(1)}, f32[32,108]{1,0:T(8,128)S(1)}) custom-call(bf16[7,8,8,16]{3,2,1,0:T(8,128)(2,1)} %fields_h.1, s32[8,8,16]{2,1,0:T(8,128)} %ids_h.1, bf16[64,128]{1,0:T(8,128)(2,1)} %bitcast.7, bf16[7,64]{1,0:T(8,128)(2,1)} %bitcast.8, bf16[64,1728]{1,0:T(8,128)(2,1)} %k_fine_h.1, ...), custom_call_target="tpu_custom_call" | custom-call | tf_op jit(solution)/shard_map/pallas_call | solution.py:743
  57.4 0.7 %shard_map.104 = (bf16[32,4,8,32]{3,2,1,0:T(8,128)(2,1)}, f32[16,54]{1,0:T(8,128)}, f32[32,108]{1,0:T(8,128)}) custom-call(bf16[32,4,8,32]{3,2,1,0:T(8,128)(2,1)S(1)} %get-tuple-element.9.a, f32[16,54]{1,0:T(8,128)S(1)} %get-tuple-element.10.b, f32[32,108]{1,0:T(8,128)S(1)} %get-tuple-element.11.c), custom_call_target="tpu_custom_call" | custom-call | tf_op jit(solution)/shard_map/pallas_call | solution.py:757

commit v5 on v4

--- a/solution.py
+++ b/solution.py
@@ -113,6 +113,11 @@
     downs,
     downr,
     dsum,
+    dpart,
+    bds,
+    bdr,
+    b2s,
+    b2r,
     gball,
     gbs,
     gbr,
@@ -137,6 +142,10 @@
     r7,
     s8,
     r8,
+    s9,
+    r9,
+    s10,
+    r10,
 ):
     nx, ny, nz = sizes
     gx, gy, gz = lax.axis_index("gx"), lax.axis_index("gy"), lax.axis_index("gz")
@@ -149,7 +158,8 @@
     near = [n for n in near if n != (0, 0, 0)]
     columns = [(dx, 0, 0) for dx in range(1, nx)]
     planes = [(0, dy, dz) for dy in range(ny) for dz in range(nz) if (dy, dz) != (0, 0)]
-    partners = sorted({(a % nx, b % ny, c % nz) for a, b, c in near + columns + planes})
+    sheets = [(dx, dy, 0) for dx in range(nx) for dy in range(ny) if (dx, dy) != (0, 0)]
+    partners = sorted({(a % nx, b % ny, c % nz) for a, b, c in near + columns + planes + sheets})
     partners.sort(key=lambda p: -2 * min(p[1], ny - p[1]) - min(p[2], nz - p[2]) - min(p[0], nx - p[0]))
     barrier = pltpu.get_barrier_semaphore()
     for p in partners:
@@ -574,7 +584,9 @@
     grad_down_t = jnp.transpose(grad_down).astype(BF16)
 
     part = dot(grad_down_t, ad[...]) * scale
-    downs[...] = part.reshape(nx, 16, 1792).astype(BF16)
+    part = part.reshape(nx, 16, 1792)
+    downs[...] = part[:, 0:8].astype(BF16)
+    dpart[...] = part[:, 8:16].reshape(8 * nx, 1792)
     down_copies = []
     for k in range(1, nx):
         target = lax.rem(gx + k, nx)
@@ -590,6 +602,27 @@
         )
     for c in down_copies:
         c.start()
+
+    low_half = lane_iota((8 * nx, 128)) < 64
+    for k in range(ny * nz // 2):
+        tz, pair = k % nz, k // nz
+        low = piece(lambda tile: dpart[:, tile * 128 : tile * 128 + 128], 54 * (2 * pair * nz + tz), 54)
+        high = 54 * ((2 * pair + 1) * nz + tz) - 64
+        high = piece(lambda tile: dpart[:, tile * 128 : tile * 128 + 128], high, 118)
+        bds[tz, pair] = jnp.where(low_half, low, high).reshape(nx, 8, 128).astype(BF16)
+    bd_copies = []
+    for k in range(1, nz):
+        target = lax.rem(gz + k, nz)
+        c = pltpu.make_async_remote_copy(
+            src_ref=bds.at[target],
+            dst_ref=bdr.at[gz],
+            send_sem=s9.at[k],
+            recv_sem=r9.at[k],
+            device_id=(gx, gy, target),
+            device_id_type=MESH,
+        )
+        c.start()
+        bd_copies.append(c)
 
     total = gbs[gz].astype(F32)
     for k, c in enumerate(gb_copies, 1):
@@ -614,11 +647,8 @@
     for k, c in enumerate(down_copies, 1):
         c.wait()
         dsum[...] += downr[lax.rem(gx - k + nx, nx)].astype(F32)
-    low_half = lane_iota((8, 128)) < 64
     for k in range(ny * nz):
-        cut = piece(lambda tile: dsum[:, tile * 128 : tile * 128 + 128], 54 * k, 54)
-        cut = jnp.where(low_half, cut[0:8], pltpu.roll(cut[8:16], 64, 1))
-        gds[k] = cut.astype(BF16)
+        gds[k] = piece(lambda tile: dsum[:, tile * 128 : tile * 128 + 128], 54 * k, 54).astype(BF16)
     gd_copies = []
     planes.sort(key=lambda p: -2 * min(p[1], ny - p[1]) - min(p[2], nz - p[2]))
     for k, (_, dy, dz) in enumerate(planes):
@@ -633,6 +663,25 @@
         )
         c.start()
         gd_copies.append(c)
+    total = bds[gz].astype(F32)
+    for k, c in enumerate(bd_copies, 1):
+        c.wait()
+        total = total + bdr[lax.rem(gz - k + nz, nz)].astype(F32)
+    b2s[...] = total.astype(BF16)
+    sheets.sort(key=lambda p: -2 * min(p[1], ny - p[1]) - min(p[0], nx - p[0]))
+    b2_copies = []
+    for k, (dx, dy, _) in enumerate(sheets):
+        tx, ty = lax.rem(gx + dx, nx), lax.rem(gy + dy, ny)
+        c = pltpu.make_async_remote_copy(
+            src_ref=b2s.at[ty // 2, tx],
+            dst_ref=b2r.at[gx * ny + gy],
+            send_sem=s10.at[k],
+            recv_sem=r10.at[k],
+            device_id=(tx, ty, gz),
+            device_id_type=MESH,
+        )
+        c.start()
+        b2_copies.append(c)
     total = gb2s[gy].astype(F32)
     for k, c in enumerate(gb2_copies, 1):
         c.wait()
@@ -645,7 +694,14 @@
         source = lax.rem(gy - dy + ny, ny) * nz + lax.rem(gz - dz + nz, nz)
         total = total + gdr[source].astype(F32)
     gdown_o[0:8, :] = total[:, 0:54]
-    gdown_o[8:16, :] = pltpu.roll(total, 64, 1)[:, 0:54]
+    total = b2s[gy // 2, gx].astype(F32)
+    for c in b2_copies:
+        c.wait()
+    for k, (dx, dy, _) in enumerate(sheets):
+        source = lax.rem(gx - dx + nx, nx) * ny + lax.rem(gy - dy + ny, ny)
+        total = total + b2r[source].astype(F32)
+    total = jnp.where(lax.rem(gy, 2) == 1, pltpu.roll(total, 64, 1), total)
+    gdown_o[8:16, :] = total[:, 0:54]
 
 
 def put_out(a, b, c, a_out, b_out, c_out, sems):
@@ -712,9 +768,14 @@
         V((2, 256, 1792), BF16),
         V((nx, 128, 128), BF16),
         V((nx, 128, 128), BF16),
-        V((nx, 16, 1792), BF16),
-        V((nx, 16, 1792), BF16),
-        V((16, 1792), F32),
+        V((nx, 8, 1792), BF16),
+        V((nx, 8, 1792), BF16),
+        V((8, 1792), F32),
+        V((8 * nx, 1792), F32),
+        V((nz, ny // 2, nx, 8, 128), BF16),
+        V((nz, ny // 2, nx, 8, 128), BF16),
+        V((ny // 2, nx, 8, 128), BF16),
+        V((nx * ny, 8, 128), BF16),
         V((96, 1152), F32),
         V((nz, ny, 32, 128), BF16),
         V((nz, ny, 32, 128), BF16),
@@ -739,6 +800,10 @@
         D((n,)),
         D((ny,)),
         D((ny,)),
+        D((nz,)),
+        D((nz,)),
+        D((nx * ny,)),
+        D((nx * ny,)),
     ]
     bottle, grad_down, grad_bottle = pl.pallas_call(
         functools.partial(body, sizes),

time: 58.2 us -> 57.1 us (0.981)
  Pallas kernels: 57.5 us -> 56.4 us
    pallas_call x1, Pallas kernels: 56.8 us -> 55.6 us  [per_device(): pl.pallas_call(functools.partial(body, sizes), out_shape=(V((32, 4, 8, 32...]
where the time goes in v5:
time: 57.1 us; the launch traced here: 57 us
  Pallas kernels  56.4 us (99%)
  between operations  0.64 us (1%)
    pallas_call x1, Pallas kernels, per_device(): pl.pallas_call(functools.partial(body, sizes), out_shape=(V((32, 4, 8, 32...  55.6 us

profile of v5, /device:TPU:1, one launch (start us, length us, event | category | flops | bytes accessed | tf_op | source)
XLA Modules:
  0.0 57.0 jit_solution(307792828881978867)
XLA Ops:
  0.6 55.6 %shard_map.103 = (bf16[32,4,8,32]{3,2,1,0:T(8,128)(2,1)S(1)}, f32[16,54]{1,0:T(8,128)S(1)}, f32[32,108]{1,0:T(8,128)S(1)}) custom-call(bf16[7,8,8,16]{3,2,1,0:T(8,128)(2,1)} %fields_h.1, s32[8,8,16]{2,1,0:T(8,128)} %ids_h.1, bf16[64,128]{1,0:T(8,128)(2,1)} %bitcast.7, bf16[7,64]{1,0:T(8,128)(2,1)} %bitcast.8, bf16[64,1728]{1,0:T(8,128)(2,1)} %k_fine_h.1, ...), custom_call_target="tpu_custom_call" | custom-call | tf_op jit(solution)/shard_map/pallas_call | solution.py:808
  56.3 0.7 %shard_map.104 = (bf16[32,4,8,32]{3,2,1,0:T(8,128)(2,1)}, f32[16,54]{1,0:T(8,128)}, f32[32,108]{1,0:T(8,128)}) custom-call(bf16[32,4,8,32]{3,2,1,0:T(8,128)(2,1)S(1)} %get-tuple-element.9.a, f32[16,54]{1,0:T(8,128)S(1)} %get-tuple-element.10.b, f32[32,108]{1,0:T(8,128)S(1)} %get-tuple-element.11.c), custom_call_target="tpu_custom_call" | custom-call | tf_op jit(solution)/shard_map/pallas_call | solution.py:822

commit v6 on v5

--- a/solution.py
+++ b/solution.py
@@ -159,7 +159,7 @@
     columns = [(dx, 0, 0) for dx in range(1, nx)]
     planes = [(0, dy, dz) for dy in range(ny) for dz in range(nz) if (dy, dz) != (0, 0)]
     sheets = [(dx, dy, 0) for dx in range(nx) for dy in range(ny) if (dx, dy) != (0, 0)]
-    partners = sorted({(a % nx, b % ny, c % nz) for a, b, c in near + columns + planes + sheets})
+    partners = sorted({(a % nx, b % ny, c % nz) for a, b, c in near + columns + [(0, 0, nz // 2)]})
     partners.sort(key=lambda p: -2 * min(p[1], ny - p[1]) - min(p[2], nz - p[2]) - min(p[0], nx - p[0]))
     barrier = pltpu.get_barrier_semaphore()
     for p in partners:

time: 57.1 us -> 56.5 us (0.989)
  Pallas kernels: 56.4 us -> 55.7 us
    pallas_call x1, Pallas kernels: 55.6 us -> 55 us  [per_device(): pl.pallas_call(functools.partial(body, sizes), out_shape=(V((32, 4, 8, 32...]
where the time goes in v6:
time: 56.5 us; the launch traced here: 56.4 us
  Pallas kernels  55.7 us (99%)
  between operations  0.64 us (1%)
    pallas_call x1, Pallas kernels, per_device(): pl.pallas_call(functools.partial(body, sizes), out_shape=(V((32, 4, 8, 32...  55 us

profile of v6, /device:TPU:1, one launch (start us, length us, event | category | flops | bytes accessed | tf_op | source)
XLA Modules:
  0.0 56.4 jit_solution(6138333498316885438)
XLA Ops:
  0.6 55.0 %shard_map.103 = (bf16[32,4,8,32]{3,2,1,0:T(8,128)(2,1)S(1)}, f32[16,54]{1,0:T(8,128)S(1)}, f32[32,108]{1,0:T(8,128)S(1)}) custom-call(bf16[7,8,8,16]{3,2,1,0:T(8,128)(2,1)} %fields_h.1, s32[8,8,16]{2,1,0:T(8,128)} %ids_h.1, bf16[64,128]{1,0:T(8,128)(2,1)} %bitcast.7, bf16[7,64]{1,0:T(8,128)(2,1)} %bitcast.8, bf16[64,1728]{1,0:T(8,128)(2,1)} %k_fine_h.1, ...), custom_call_target="tpu_custom_call" | custom-call | tf_op jit(solution)/shard_map/pallas_call | solution.py:808
  55.6 0.7 %shard_map.104 = (bf16[32,4,8,32]{3,2,1,0:T(8,128)(2,1)}, f32[16,54]{1,0:T(8,128)}, f32[32,108]{1,0:T(8,128)}) custom-call(bf16[32,4,8,32]{3,2,1,0:T(8,128)(2,1)S(1)} %get-tuple-element.9.a, f32[16,54]{1,0:T(8,128)S(1)} %get-tuple-element.10.b, f32[32,108]{1,0:T(8,128)S(1)} %get-tuple-element.11.c), custom_call_target="tpu_custom_call" | custom-call | tf_op jit(solution)/shard_map/pallas_call | solution.py:822

commit v7 on v6

--- a/solution.py
+++ b/solution.py
@@ -155,7 +155,7 @@
         return (lax.rem(gx + dx + nx, nx), lax.rem(gy + dy + ny, ny), lax.rem(gz + dz + nz, nz))
 
     near = [(dx, dy, dz) for dx in (-1, 0, 1) for dy in (-1, 0, 1) for dz in (-1, 0, 1)]
-    near = [n for n in near if n != (0, 0, 0)]
+    near = sorted([n for n in near if n != (0, 0, 0)], key=lambda n: abs(n[0]))
     columns = [(dx, 0, 0) for dx in range(1, nx)]
     planes = [(0, dy, dz) for dy in range(ny) for dz in range(nz) if (dy, dz) != (0, 0)]
     sheets = [(dx, dy, 0) for dx in range(nx) for dy in range(ny) if (dx, dy) != (0, 0)]
@@ -319,8 +319,11 @@
 
     half_rows = lane_iota((312, 128)) < 64
 
+    def spread_planes(e, carry):
+        spread_plane(e)
+        return carry
+
     def next_plane(x, carry):
-        spread_plane(x + 2)
         fine_plane(x)
         return carry
 
@@ -365,20 +368,21 @@
         sb[gx, x] = cb[x].astype(BF16)
         for k in range(1, nx):
             coarse_copy(x, k).start()
+
+        @pl.when(x < 3)
+        def _():
+            lax.fori_loop(2 * x + 5, 2 * x + 7, spread_planes, 0)
+
         return carry
 
     embed(range(2, 10))
-    spread_plane(2)
+    lax.fori_loop(2, 5, spread_planes, 0)
     for c, n in zip(halo, near):
         if n[0] != 0:
             c.wait()
     embed((0, 1, 10))
 
-    def first_planes(e, carry):
-        spread_plane(e)
-        return carry
-
-    lax.fori_loop(0, 2, first_planes, 0)
+    lax.fori_loop(0, 2, spread_planes, 0)
     fine_plane(0)
     lax.fori_loop(0, 4, coarse_plane, 0)
 

time: 56.5 us -> 56.8 us (level)
  no operation moved by 1% of the time
where the time goes in v7:
time: 56.8 us; the launch traced here: 56.6 us
  Pallas kernels  56 us (99%)
  between operations  0.64 us (1%)
    pallas_call x1, Pallas kernels, per_device(): pl.pallas_call(functools.partial(body, sizes), out_shape=(V((32, 4, 8, 32...  55.3 us

profile of v7, /device:TPU:1, one launch (start us, length us, event | category | flops | bytes accessed | tf_op | source)
XLA Modules:
  0.0 56.6 jit_solution(11643776320321230459)
XLA Ops:
  0.6 55.3 %shard_map.103 = (bf16[32,4,8,32]{3,2,1,0:T(8,128)(2,1)S(1)}, f32[16,54]{1,0:T(8,128)S(1)}, f32[32,108]{1,0:T(8,128)S(1)}) custom-call(bf16[7,8,8,16]{3,2,1,0:T(8,128)(2,1)} %fields_h.1, s32[8,8,16]{2,1,0:T(8,128)} %ids_h.1, bf16[64,128]{1,0:T(8,128)(2,1)} %bitcast.7, bf16[7,64]{1,0:T(8,128)(2,1)} %bitcast.8, bf16[64,1728]{1,0:T(8,128)(2,1)} %k_fine_h.1, ...), custom_call_target="tpu_custom_call" | custom-call | tf_op jit(solution)/shard_map/pallas_call | solution.py:812
  55.9 0.7 %shard_map.104 = (bf16[32,4,8,32]{3,2,1,0:T(8,128)(2,1)}, f32[16,54]{1,0:T(8,128)}, f32[32,108]{1,0:T(8,128)}) custom-call(bf16[32,4,8,32]{3,2,1,0:T(8,128)(2,1)S(1)} %get-tuple-element.9.a, f32[16,54]{1,0:T(8,128)S(1)} %get-tuple-element.10.b, f32[32,108]{1,0:T(8,128)S(1)} %get-tuple-element.11.c), custom_call_target="tpu_custom_call" | custom-call | tf_op jit(solution)/shard_map/pallas_call | solution.py:826
